TPU v7x, 256 devices: a whole 4x4x8 slice. The times are simulated.
256 devices in a mesh: lon: 16 (over y, z_lo, core), lat: 16 (over x, z_hi).
Axes of the slice: x: 4, y: 4, z: 8 (z_hi: 4, z_lo: 2; z = z_hi * 2 + z_lo), core: 2. Of those that a mesh axis runs over, the one named last changes fastest.
Arguments:
- fine_state: bfloat16 [2048, 1024, 128], P('lon', 'lat'), may hold values from -6 to 6
- coarse_state: bfloat16 [128, 64, 512], P('lon', 'lat'), may hold values from -6 to 6
- norm_gains: float32 [2, 128], replicated, may hold values from 0.25 to 1.75
- kernels: bfloat16 [2, 3, 3, 128, 128], replicated, may hold values from -0.1875 to 0.1875
- token_gain: float32 [512], replicated, may hold values from 0.25 to 1.75
- head_gains: float32 [2, 64], replicated, may hold values from 1.2 to 2.2
- query_weight: bfloat16 [512, 512], replicated, may hold values from -0.25 to 0.25
- keyvalue_weight: bfloat16 [512, 1024], replicated, may hold values from -0.25 to 0.25
- output_weight: bfloat16 [512, 512], replicated, may hold values from -0.25 to 0.25
- expand_weight: bfloat16 [512, 128], replicated, may hold values from -0.25 to 0.25
Outputs:
- fine_result: bfloat16 [2048, 1024, 128], P('lon', 'lat')
- coarse_result: bfloat16 [128, 64, 512], P('lon', 'lat')
All inputs are finite; a program needn't handle non-finite values.
Results may differ from a plain program's by a relative error of at most 0.005.
Values may be sent and summed in bfloat16 or wider, within the bound.
No kernel may reach another device: no remote copies, remote signals or barrier semaphores. Data moves between devices by JAX's collectives and lax.ppermute only.
A program may use at most 192 MiB of HBM per device.

v0:
```python
import math

import jax
import jax.numpy as jnp
from jax import lax
from jax.sharding import PartitionSpec as P


def padded_2(block, sides, width, periodic):
    for axis, dim in sides:
        count = lax.axis_size(axis)
        forward = [(i, i + 1) for i in range(count - 1)]
        if periodic:
            forward.append((count - 1, 0))
        backward = [(target, source) for source, target in forward]
        low = lax.ppermute(
            lax.slice_in_dim(block, block.shape[dim] - width, None, axis=dim), axis, forward
        )
        high = lax.ppermute(lax.slice_in_dim(block, 0, width, axis=dim), axis, backward)
        block = jnp.concatenate([low, block, high], axis=dim)
    return block


def rescale_rows(matrix, gain_row):
    return matrix * lax.rsqrt(jnp.mean(matrix * matrix, axis=-1, keepdims=True) + 1e-06) * gain_row


def rescale_heads(projected, gain_row):
    shaped = projected.reshape(projected.shape[0], -1, gain_row.shape[0])
    return rescale_rows(shaped, gain_row)


def convolve(padded, kernel):
    return lax.conv_general_dilated(
        padded[None],
        kernel,
        (1, 1),
        "VALID",
        dimension_numbers=("NHWC", "HWIO", "NHWC"),
        preferred_element_type=jnp.float32,
    )[0]


def attach_rims(hidden, rim_width):
    wrapped = padded_2(hidden, (("lon", 0),), rim_width, True)
    return padded_2(wrapped, (("lat", 1),), rim_width, False)


def local(
    fine_state,
    coarse_state,
    norm_gains,
    kernels,
    token_gain,
    head_gains,
    query_weight,
    keyvalue_weight,
    output_weight,
    expand_weight,
):
    width_all = query_weight.shape[0]
    head_size = head_gains.shape[1]
    head_count = width_all // head_size
    lon_tokens = coarse_state.shape[0]
    lat_tokens = coarse_state.shape[1]
    lon_cells, lat_cells, channels = fine_state.shape
    first_hidden = jax.nn.silu(rescale_rows(fine_state.astype(jnp.float32), norm_gains[0])).astype(
        jnp.bfloat16
    )
    first_output = convolve(attach_rims(first_hidden, 1), kernels[0])
    second_hidden = jax.nn.silu(rescale_rows(first_output, norm_gains[1])).astype(jnp.bfloat16)
    second_output = convolve(attach_rims(second_hidden, 1), kernels[1])
    tokens = coarse_state.reshape(-1, width_all)
    normed = rescale_rows(tokens.astype(jnp.float32), token_gain).astype(jnp.bfloat16)
    scale_factor = 1.0 / math.sqrt(head_size)
    queries = (
        rescale_heads(
            jnp.dot(normed, query_weight, preferred_element_type=jnp.float32), head_gains[0]
        )
        * scale_factor
    ).astype(jnp.bfloat16)
    projected = jnp.dot(normed, keyvalue_weight, preferred_element_type=jnp.float32)
    key_rows = (
        rescale_heads(projected[:, :width_all], head_gains[1])
        .astype(jnp.bfloat16)
        .reshape(-1, width_all)
    )
    value_rows = projected[:, width_all:].astype(jnp.bfloat16)
    key_rows, value_rows = (key_rows, value_rows)
    accumulate_key_rows = lax.all_gather(key_rows, ("lon", "lat"), axis=0, tiled=True)
    accumulate_value_rows = lax.all_gather(value_rows, ("lon", "lat"), axis=0, tiled=True)
    key_heads = accumulate_key_rows.reshape(accumulate_key_rows.shape[0], head_count, head_size)
    value_heads = accumulate_value_rows.reshape(
        accumulate_value_rows.shape[0], head_count, head_size
    )
    scores = jnp.einsum("thd,shd->hts", queries, key_heads, preferred_element_type=jnp.float32)
    weights = jnp.exp(scores)
    totals = jnp.sum(weights, axis=-1)
    summed = jnp.einsum(
        "hts,shd->thd",
        weights.astype(jnp.bfloat16),
        value_heads,
        preferred_element_type=jnp.float32,
    )
    summed, totals = (summed, totals)
    attended = (
        (summed / jnp.transpose(totals)[:, :, None]).reshape(-1, width_all).astype(jnp.bfloat16)
    )
    coarse_result = (
        tokens.astype(jnp.float32)
        + jnp.dot(attended, output_weight, preferred_element_type=jnp.float32)
    ).astype(jnp.bfloat16)
    lifted = jnp.dot(coarse_result, expand_weight, preferred_element_type=jnp.float32).reshape(
        lon_tokens, 1, lat_tokens, 1, channels
    )
    merged = (fine_state.astype(jnp.float32) + second_output).reshape(
        lon_tokens, lon_cells // lon_tokens, lat_tokens, lat_cells // lat_tokens, channels
    ) + lifted
    fine_result = merged.reshape(lon_cells, lat_cells, channels).astype(jnp.bfloat16)
    return (fine_result, coarse_result.reshape(lon_tokens, lat_tokens, width_all))


def solution(mesh):
    return jax.shard_map(
        local,
        mesh=mesh,
        in_specs=(
            P("lon", "lat", None),
            P("lon", "lat", None),
            P(),
            P(),
            P(),
            P(),
            P(),
            P(),
            P(),
            P(),
        ),
        out_specs=(P("lon", "lat", None), P("lon", "lat", None)),
        check_vma=False,
    )
```

profile of v0, /device:TPU:99, one launch (start us, length us, event | category | flops | bytes accessed | tf_op | source)
XLA Modules:
  0.0 1499.1 jit_solution(16317238744384808810)
XLA Ops:
  13.6 3.4 fusion.2
  17.1 3.4 fusion.9
  21.3 2.0 collective-permute-start
  23.3 1.8 collective-permute-done.1
  25.1 1.9 collective-permute-start.3
  27.0 5.7 collective-permute-start.2
  34.7 1.7 maximum_bitcast_fusion
  37.5 5.7 broadcast_select_fusion.1
  46.8 1.6 collective-permute-start.5
  48.4 2.2 collective-permute-start.4
  52.4 6.7 collective-permute-start.7
  59.0 2.1 collective-permute-start.6
  61.2 3.5 collective-permute-done.6
  64.7 1.8 maximum_bitcast_fusion.1
  67.1 5.7 broadcast_select_fusion
  72.8 3.0 copy.50
  75.8 665.4 %all-gather.5.cloned.1.call-done = bf16[8192,512]{1,0:T(8,128)(2,1)} async-done(((bf16[32,512]{1,0:T(8,128)(2,1)}), bf16[8192,512]{1,0:T(8,128)(2,1)}) %all-gather.5.cloned.1.call-update) | async-done | bytes 8388624 | tf_op jit(solution)/shard_map/all_gather | solution.py:90
  741.2 12.0 copy.55
  753.2 7.0 fusion.63
  760.2 705.3 %all-gather.3.cloned.1.call-done = bf16[8192,512]{1,0:T(8,128)(2,1)} async-done(((bf16[32,512]{1,0:T(8,128)(2,1)}), bf16[8192,512]{1,0:T(8,128)(2,1)}) %all-gather.3.cloned.1.call-update) | async-done | bytes 8388624 | tf_op jit(solution)/shard_map/all_gather | solution.py:91
  1465.4 11.6 copy.51
  1477.0 6.9 fusion.41
  1485.6 4.0 fusion.11
  1489.6 2.7 copy.58
  (77 shorter events, 17.7 us)
Async XLA Ops:
  7.2 1.9 copy-start
  7.2 734.0 %all-gather.5.cloned.1.call-start = ((), (), s32[]{:S(2)}) async-start(), calls=%async_computation.1 | async-start | bytes 8421376 | tf_op jit(solution)/shard_map/all_gather | solution.py:90
  12.1 1453.3 %all-gather.3.cloned.1.call-start = ((), (), s32[]{:S(2)}) async-start(), calls=%async_computation | async-start | bytes 8421376 | tf_op jit(solution)/shard_map/all_gather | solution.py:91
  13.6 19.1 %copy-start.5 = (bf16[8,4,512]{2,1,0:T(4,128)(2,1)S(1)}, bf16[8,4,512]{2,1,0:T(4,128)(2,1)}, u32[]{:S(2)}) copy-start(bf16[8,4,512]{2,1,0:T(4,128)(2,1)} %param.11) | copy-start | bytes 98308
  13.6 19.1 %copy-start.7 = (f32[512]{0:T(512)S(1)}, f32[512]{0:T(512)}, u32[]{:S(2)}) copy-start(f32[512]{0:T(512)} %param.14) | copy-start | bytes 6148
  13.6 19.2 %copy-start.4 = (bf16[512,512]{1,0:T(8,128)(2,1)S(1)}, bf16[512,512]{1,0:T(8,128)(2,1)}, u32[]{:S(2)}) copy-start(bf16[512,512]{1,0:T(8,128)(2,1)} %param.16) | copy-start | bytes 1572868
  20.6 4.5 collective-permute-start.1
  21.3 3.7 collective-permute-start
  25.1 7.9 collective-permute-start.3
  27.0 7.6 collective-permute-start.2
  36.4 1.1 copy-start.8
  36.4 1.1 copy-start.9
  46.8 5.5 collective-permute-start.5
  48.4 3.9 collective-permute-start.4
  52.4 8.8 collective-permute-start.7
  59.0 5.7 collective-permute-start.6
  1477.0 7.1 copy-start.3
  1477.0 7.9 copy-start.6
  1484.0 1.6 copy-start.2
  1485.6 6.7 copy-start.1
Sparse Core Ops, SparseCore 0:
  12.2 728.9 all-gather.4
  743.6 721.7 all-gather.2
where the time goes:
time: 1500 us
  waiting for transfers between devices  1380 us (92%)
  local copies, waits for them, and re-layouts  37 us (2%)
  matrix products  27 us (2%)
  starting transfers between devices  23 us (2%)
  other arithmetic  18.8 us (1%)
    all_gather x1, waiting for transfers between devices, local(): lax.all_gather(value_rows, ('lon', 'lat'), axis=0, tiled=True)  705 us
    all_gather x1, waiting for transfers between devices, local(): lax.all_gather(key_rows, ('lon', 'lat'), axis=0, tiled=True)  665 us
  transfers between devices with their start and end apart: 10, of which 6 were waited for; matrix products, arithmetic and copies ran while one was open for 3% of the time, Pallas kernels for 0%

commit v1 on v0

v1 whole, which is shorter than its diff:
```python
import functools
import math
import jax
import jax.numpy as jnp
from jax import lax
from jax.experimental import pallas as pl
from jax.experimental.pallas import tpu as pltpu

from jax.sharding import PartitionSpec as P


WIDE = 80
CIRCLE = 72
NORM_UNROLL = 2
CONV_UNROLL = 1
SHIFT_UNROLL = 4
CONV2_UNROLL = 1
F32 = jnp.float32
BF16 = jnp.bfloat16


def unit_rows(v, gain):
    return v * lax.rsqrt(jnp.mean(v * v, axis=-1, keepdims=True) + 1e-06) * gain


def silu(v):
    half = v * 0.5
    return half + half * jnp.tanh(half)


def pair_weights(taps_ref, which, pair_ref):
    zero = jnp.zeros((128, 128), BF16)
    for row in range(4):
        for b in range(3):
            at = (row * 3 + b) * 128
            pair_ref[at : at + 128, 0:128] = taps_ref[which, row, b] if row < 3 else zero
            pair_ref[at : at + 128, 128:256] = taps_ref[which, row - 1, b] if row > 0 else zero


def store_shifted(hidden_ref, p, value, width):
    hidden_ref[0, p, :, :width] = pltpu.roll(value, 1, 1)[:, :width].astype(BF16)
    hidden_ref[1, p, :, :width] = value[:, :width].astype(BF16)
    hidden_ref[2, p, :, :width] = pltpu.roll(value, CIRCLE - 1, 1)[:, :width].astype(BF16)


def conv_pairs(hidden_ref, pair_ref, first, count, width):
    pieces = []
    for row in range(4):
        for b in range(3):
            piece = hidden_ref[b, pl.ds(first + row // 2, count), row % 2]
            pieces.append(piece.reshape(count * width, 128))
    return jnp.dot(
        jnp.concatenate(pieces, axis=1), pair_ref[...], preferred_element_type=F32
    )


def first_conv_kernel(begin, count, fine_ref, low_ref, high_ref, rim_ref, taps_ref, gains_ref, inside_ref, out_ref, hidden_ref, pair_ref):
    pair_weights(taps_ref, 0, pair_ref)
    gain = gains_ref[0:1, :].reshape(1, 1, 128)

    def activate(main, rim, p):
        row = jnp.concatenate([main.astype(F32), rim.astype(F32)], axis=1)
        store_shifted(hidden_ref, p - begin, silu(unit_rows(row, gain)), CIRCLE)

    lower, upper = begin, begin + count + 1
    if lower == 0:
        activate(low_ref[...], rim_ref[0:2], 0)
        lower = 1
    if upper == 66:
        activate(high_ref[...], rim_ref[130:132], 65)
        upper = 65

    def norm_step(p, carry):
        activate(fine_ref[pl.ds(2 * p - 2, 2)], rim_ref[pl.ds(2 * p, 2)], p)
        return carry

    lax.fori_loop(lower, upper, norm_step, 0, unroll=NORM_UNROLL)
    second_gain = gains_ref[1:2, :].reshape(1, 1, 128)
    inside = inside_ref[...].reshape(1, CIRCLE, 128)

    def conv_step(i, carry):
        first = i * 5
        both = conv_pairs(hidden_ref, pair_ref, first, 5, WIDE)
        for half in range(2):
            value = both[:, 128 * half : 128 * half + 128].reshape(5, WIDE, 128)[:, :CIRCLE]
            value = silu(unit_rows(value, second_gain)) * inside
            out_ref[pl.ds(first, 5), half] = value.astype(BF16)
        return carry

    lax.fori_loop(0, count // 5, conv_step, 0, unroll=CONV_UNROLL)


VMEM_SPEC = pl.BlockSpec(memory_space=pltpu.VMEM)


def first_conv(begin, count, fine, low, high, rim, kernels, gains, inside):
    return pl.pallas_call(
        functools.partial(first_conv_kernel, begin, count),
        out_shape=jax.ShapeDtypeStruct((count, 2, CIRCLE, 128), BF16),
        in_specs=[VMEM_SPEC] * 7,
        out_specs=VMEM_SPEC,
        scratch_shapes=[pltpu.VMEM((3, count + 1, 2, WIDE, 128), BF16), pltpu.VMEM((1536, 256), BF16)],
        compiler_params=pltpu.CompilerParams(vmem_limit_bytes=14 << 20),
        name="first_conv",
    )(fine, low, high, rim, kernels, gains, inside)


def second_conv_kernel(begin, pairs, split_at, *refs):
    hidden_refs, (taps_ref, fine_ref, out_ref, hidden_ref, pair_ref) = refs[:-5], refs[-5:]
    pair_weights(taps_ref, 1, pair_ref)
    lower = begin
    for ref, stop, offset in zip(hidden_refs, (split_at, begin + pairs + 1), (0, split_at)):
        upper = min(stop, begin + pairs + 1)

        def shift_step(p, carry, ref=ref, offset=offset):
            store_shifted(hidden_ref, p - begin, ref[p - offset].astype(F32), 64)
            return carry

        if upper > lower:
            lax.fori_loop(lower, upper, shift_step, 0, unroll=SHIFT_UNROLL)
            lower = upper

    def conv_step(i, carry):
        first = i * 8
        both = conv_pairs(hidden_ref, pair_ref, first, 8, 64)
        for half in range(2):
            value = both[:, 128 * half : 128 * half + 128].reshape(8, 64, 128)
            out_ref[pl.ds(first, 8), half] = value + fine_ref[pl.ds(begin + first, 8), half].astype(F32)
        return carry

    lax.fori_loop(0, pairs // 8, conv_step, 0, unroll=CONV2_UNROLL)


def second_conv(begin, pairs, hidden, kernels, fine):
    split_at = hidden[0].shape[0]
    return pl.pallas_call(
        functools.partial(second_conv_kernel, begin, pairs, split_at),
        out_shape=jax.ShapeDtypeStruct((pairs, 2, 64, 128), F32),
        in_specs=[VMEM_SPEC] * (len(hidden) + 2),
        out_specs=VMEM_SPEC,
        scratch_shapes=[pltpu.VMEM((3, pairs + 1, 2, 64, 128), BF16), pltpu.VMEM((1536, 256), BF16)],
        compiler_params=pltpu.CompilerParams(vmem_limit_bytes=12 << 20),
        name="second_conv",
    )(*hidden, kernels, fine.reshape(64, 2, 64, 128))


def high_low(v):
    high = v.astype(BF16)
    return high, (v - high.astype(F32)).astype(BF16)


def attention_kernel(q0_ref, q1_ref, k0_ref, k1_ref, k2_ref, k3_ref, gain_ref, head_ref, wq_ref, wkv_ref, keep_ref, send_ref):
    gain = gain_ref[...]
    lane = lax.broadcasted_iota(jnp.int32, (1, 128), 1)
    r = lax.broadcasted_iota(jnp.int32, (256, 128), 0)
    c = lax.broadcasted_iota(jnp.int32, (256, 128), 1)
    block = jnp.where(((r % 128) // 64) == (c // 64), 1.0 / 64, 0.0).astype(BF16)
    even = lane < 64

    def head_norm(v, head_gain):
        high, low = high_low(v * v)
        mean = jnp.dot(jnp.concatenate([high, low], axis=1), block, preferred_element_type=F32)
        return v * lax.rsqrt(mean + 1e-06) * head_gain

    query_rows = jnp.concatenate([q0_ref[...], q1_ref[...]], axis=0).astype(F32)
    query_rows = unit_rows(query_rows, gain).astype(BF16)
    key_rows = jnp.concatenate([k0_ref[...], k1_ref[...], k2_ref[...], k3_ref[...]], axis=0).astype(F32)
    key_rows = unit_rows(key_rows, gain).astype(BF16)
    scale = 1.0 / math.sqrt(64)
    totals = jnp.zeros((512, 128), F32)
    for g in range(4):
        at = 128 * g
        q = jnp.dot(query_rows, wq_ref[:, at : at + 128], preferred_element_type=F32)
        q = (head_norm(q, head_ref[0:1, :]) * scale).astype(BF16)
        k = jnp.dot(key_rows, wkv_ref[:, at : at + 128], preferred_element_type=F32)
        k = head_norm(k, head_ref[1:2, :])
        v = jnp.dot(key_rows, wkv_ref[:, 512 + at : 640 + at], preferred_element_type=F32)
        parts = []
        for side in range(2):
            own = even if side == 0 else jnp.logical_not(even)
            k_own = jnp.where(own, k, 0.0).astype(BF16)
            v_own = jnp.where(own, v, 1.0).astype(BF16)
            scores = lax.dot_general(q, k_own, (((1,), (1,)), ((), ())), preferred_element_type=F32)
            weights = jnp.exp(scores).astype(BF16)
            parts.append(jnp.dot(weights, v_own, preferred_element_type=F32))
        summed = jnp.where(even, parts[0], parts[1])
        total = jnp.where(even, parts[1], parts[0])
        high = total.astype(BF16).astype(F32)
        totals = totals + jnp.where(lane % 64 == 2 * g, high, jnp.where(lane % 64 == 2 * g + 1, total - high, 0.0))
        keep_ref[:, at : at + 128] = summed[0:256]
        send_ref[:, at : at + 128] = summed[256:512].astype(BF16)
    keep_ref[:, 512:640] = totals[0:256]
    send_ref[:, 512:640] = totals[256:512].astype(BF16)


def attention(q0, q1, ks, token_gain, head_gains, wq, wkv):
    full = lambda shape: pl.BlockSpec(shape, lambda: (0,) * len(shape))
    head2 = jnp.concatenate([head_gains, head_gains], axis=1)
    return pl.pallas_call(
        attention_kernel,
        out_shape=(jax.ShapeDtypeStruct((256, 640), F32), jax.ShapeDtypeStruct((256, 640), BF16)),
        in_specs=[full((256, 512))] * 2 + [full((128, 512))] * 4 + [full((1, 512)), full((2, 128)), full((512, 512)), full((512, 1024))],
        out_specs=(full((256, 640)), full((256, 640))),
        compiler_params=pltpu.CompilerParams(vmem_limit_bytes=16 << 20),
        name="attention",
    )(q0, q1, *ks, token_gain.reshape(1, 512), head2, wq, wkv)


def split_totals(x):
    lane = lax.broadcasted_iota(jnp.int32, (1, 128), 1)
    total = x + pltpu.roll(x, 127, 1)
    high = total.astype(BF16).astype(F32)
    return jnp.where(lane % 2 == 0, high, pltpu.roll(total - high, 1, 1))


def reduce_kernel(keep_ref, got_ref, out_ref, send_ref):
    rows = out_ref.shape[0]
    total = keep_ref[...] + got_ref[...].astype(F32)
    out_ref[...] = total[:rows]
    send_ref[:, :512] = total[rows:, :512].astype(BF16)
    send_ref[:, 512:] = split_totals(total[rows:, 512:]).astype(BF16)


def reduce_step(keep, got, rows):
    count = keep.shape[0]
    full = lambda shape: pl.BlockSpec(shape, lambda: (0,) * len(shape))
    return pl.pallas_call(
        reduce_kernel,
        out_shape=(jax.ShapeDtypeStruct((rows, 640), F32), jax.ShapeDtypeStruct((count - rows, 640), BF16)),
        in_specs=[full((count, 640))] * 2,
        out_specs=(full((rows, 640)), full((count - rows, 640))),
        compiler_params=pltpu.CompilerParams(vmem_limit_bytes=4 << 20),
        name="reduce_step",
    )(keep, got)


def final_kernel(keep_ref, g1_ref, g2_ref, g3_ref, tokens_ref, wo_ref, we_ref, s0_ref, s1_ref, out_ref, coarse_ref, lifted_ref, block_ref, sems):
    total = keep_ref[...] + g1_ref[...].astype(F32) + g2_ref[...].astype(F32) + g3_ref[...].astype(F32)
    r = lax.broadcasted_iota(jnp.int32, (128, 512), 0)
    head = lax.broadcasted_iota(jnp.int32, (128, 512), 1) // 64
    at = jnp.where(head % 2 == 1, 0, 64) + head // 2 * 2
    pick = jnp.where((r == at) | (r == at + 1), 1.0, 0.0).astype(BF16)
    high, low = high_low(total[:, 512:])
    spread = jnp.dot(high, pick, preferred_element_type=F32) + jnp.dot(low, pick, preferred_element_type=F32)
    attended = (total[:, :512] / spread).astype(BF16)
    coarse = tokens_ref[...].astype(F32) + jnp.dot(attended, wo_ref[...], preferred_element_type=F32)
    rounded = coarse.astype(BF16)
    lifted_ref[...] = jnp.dot(rounded, we_ref[...], preferred_element_type=F32)
    for a in range(8):
        coarse_ref[a] = coarse[4 * a : 4 * a + 4].astype(BF16)
    copies = []
    for a in range(8):
        for b in range(4):
            row = lifted_ref[4 * a + b : 4 * a + b + 1, :].reshape(1, 1, 128)
            cols = slice(16 * b, 16 * b + 16)
            half_ref, at = (s0_ref, 16 * a) if a < 4 else (s1_ref, 16 * a - 64)
            block_ref[a, :, cols] = (half_ref[at : at + 16, cols] + row).astype(BF16)
        copy = pltpu.make_async_copy(block_ref.at[a], out_ref.at[pl.ds(16 * a, 16)], sems.at[a])
        copy.start()
        copies.append(copy)
    for copy in copies:
        copy.wait()


def final(keep, got, tokens, wo, we, second):
    return pl.pallas_call(
        final_kernel,
        out_shape=(jax.ShapeDtypeStruct((128, 64, 128), BF16), jax.ShapeDtypeStruct((8, 4, 512), BF16)),
        in_specs=[VMEM_SPEC] * 9,
        out_specs=(pl.BlockSpec(memory_space=pl.ANY), VMEM_SPEC),
        scratch_shapes=[pltpu.VMEM((32, 128), F32), pltpu.VMEM((8, 16, 64, 128), BF16), pltpu.SemaphoreType.DMA((8,))],
        compiler_params=pltpu.CompilerParams(vmem_limit_bytes=12 << 20),
        name="final",
    )(keep, *got, tokens, wo, we, *second)


AXES = ("lon", "lat")


def device_pairs(move):
    pairs = []
    for y in range(4):
        for zl in range(2):
            for c in range(2):
                for x in range(4):
                    for zh in range(4):
                        ty, tl, tc, tx, th = move(y, zl, c, x, zh)
                        source = ((y * 2 + zl) * 2 + c) * 16 + x * 4 + zh
                        target = (((ty % 4) * 2 + tl % 2) * 2 + tc % 2) * 16 + (tx % 4) * 4 + th % 4
                        pairs.append((source, target))
    return pairs


def move(value, y=0, low=0, core=0, x=0, high=0):
    return lax.ppermute(
        value, AXES,
        device_pairs(lambda a, b, c, d, e: (a + y, b + low, c + core, d + x, e + high)),
    )


def block(
    fine_state,
    coarse_state,
    norm_gains,
    kernels,
    token_gain,
    head_gains,
    query_weight,
    keyvalue_weight,
    output_weight,
    expand_weight,
):
    count = 16
    forward = [(i, (i + 1) % count) for i in range(count)]
    backward = [(b, a) for a, b in forward]
    low = lax.ppermute(fine_state[-2:], "lon", forward)
    high = lax.ppermute(fine_state[:2], "lon", backward)
    tokens = coarse_state.reshape(32, 512)
    far = [tokens] + [move(tokens, high=k) for k in (1, 2, 3)]
    first = jnp.concatenate([low[:, :2], fine_state[:, :2], high[:, :2]], axis=0)
    last = jnp.concatenate([low[:, -2:], fine_state[:, -2:], high[:, -2:]], axis=0)
    left = lax.ppermute(last, "lat", forward[:-1])
    right = lax.ppermute(first, "lat", backward[:-1])
    near = [tokens] + [move(tokens, y=-k) for k in (1, 2, 3)]
    rim = jnp.concatenate([right, jnp.zeros((132, 4, 128), BF16), left], axis=1)
    position = lax.broadcasted_iota(jnp.int32, (CIRCLE, 128), 0)
    column = lax.axis_index("lat") * 64 + jnp.where(position < 68, position, position - CIRCLE)
    inside = jnp.where((column >= 0) & (column < 64 * count), 1.0, 0.0).astype(F32)
    hidden_a = first_conv(0, 35, fine_state, low, high, rim, kernels, norm_gains, inside)

    far = jnp.concatenate(far, axis=0)
    key_tokens = [far] + [move(far, x=k) for k in (1, 2, 3)]
    near = jnp.concatenate(near, axis=0)
    near = jnp.concatenate([near, move(near, low=1)], axis=0)
    hidden_b = first_conv(35, 30, fine_state, low, high, rim, kernels, norm_gains, inside)
    across = move(near, core=1)
    keep, out = attention(near, across, key_tokens, token_gain, head_gains, query_weight, keyvalue_weight)
    keep, out = reduce_step(keep, move(out, core=1), 128)
    got = move(out, low=1)
    second_a = second_conv(0, 32, (hidden_a,), kernels, fine_state)
    keep, out = reduce_step(keep, got, 32)
    got = [move(out[32 * k - 32 : 32 * k], y=k) for k in (1, 2, 3)]
    second_b = second_conv(32, 32, (hidden_a, hidden_b), kernels, fine_state)
    second = [half.reshape(64, 64, 128) for half in (second_a, second_b)]
    return final(keep, got, tokens, output_weight, expand_weight, second)


def solution(mesh):
    return jax.shard_map(
        block,
        mesh=mesh,
        in_specs=(
            P("lon", "lat", None),
            P("lon", "lat", None),
            P(),
            P(),
            P(),
            P(),
            P(),
            P(),
            P(),
            P(),
        ),
        out_specs=(P("lon", "lat", None), P("lon", "lat", None)),
        check_vma=False,
    )
```

time: 1500 us -> 79.1 us (0.05)
  the two profiles are of different devices: /device:TPU:99 before, /device:TPU:10 now
where the time goes in v1:
time: 79.1 us; the launch traced here: 78.8 us
  starting transfers between devices  38.2 us (48%)
  Pallas kernels  28.2 us (36%)
  waiting for transfers between devices  5.27 us (7%)
  local copies, waits for them, and re-layouts  4.67 us (6%)
  other arithmetic  1.31 us (2%)
  between operations  1.13 us (1%)
    ppermute x16, starting transfers between devices, move(): lax.ppermute(value, AXES, device_pairs(lambda a, b, c, d, e: (a + y, b +...  28.6 us
    pallas_call x2, Pallas kernels, first_conv(): pl.pallas_call(functools.partial(first_conv_kernel, begin, count), out_sh...  13.6 us
    pallas_call x2, Pallas kernels, second_conv(): pl.pallas_call(functools.partial(second_conv_kernel, begin, pairs, split_...  6.1 us
    pallas_call x1, Pallas kernels, attention(): pl.pallas_call(attention_kernel, out_shape=(jax.ShapeDtypeStruct((256, 64...  5.72 us
    ppermute x16, waiting for transfers between devices, move(): lax.ppermute(value, AXES, device_pairs(lambda a, b, c, d, e: (a + y, b +...  5.26 us
    ppermute x1, starting transfers between devices, block(): left = lax.ppermute(last, 'lat', forward[:-1])  4.58 us
    ppermute x1, starting transfers between devices, block(): right = lax.ppermute(first, 'lat', backward[:-1])  4.27 us
    pallas_call x1, Pallas kernels, final(): pl.pallas_call(final_kernel, out_shape=(jax.ShapeDtypeStruct((128, 64, 12...  2.5 us
  transfers between devices with their start and end apart: 20, of which 2 were waited for; matrix products, arithmetic and copies ran while one was open for 4% of the time, Pallas kernels for 32%

profile of v1, /device:TPU:10, one launch (start us, length us, event | category | flops | bytes accessed | tf_op | source)
XLA Modules:
  0.0 78.8 jit_solution(2805831756928120085)
XLA Ops:
  1.5 6.4 %collective-permute-start.7 = (bf16[32,512]{1,0:T(8,128)(2,1)S(1)}, bf16[32,512]{1,0:T(8,128)(2,1)S(1)}, u32[]{:S(2)}, u32[]{:S(2)}) collective-permute-start(bf16[32,512]{1,0:T(8,128)(2,1)S(1)} %reshape.20.tokens_ref), channel_id=1, source_target_pairs={{0,3},{1,0},{2,1},{3,2},{4,7},{5,4},{6,5},{7,6},{8,11},{9,8},{10,9... | collective-permute-start | bytes 98312 | tf_op jit(solution)/shard_map/ppermute | solution.py:295
  7.9 1.0 %collective-permute-start.6 = (bf16[32,512]{1,0:T(8,128)(2,1)S(1)}, bf16[32,512]{1,0:T(8,128)(2,1)S(1)}, u32[]{:S(2)}, u32[]{:S(2)}) collective-permute-start(bf16[32,512]{1,0:T(8,128)(2,1)S(1)} %reshape.20.tokens_ref), channel_id=1, source_target_pairs={{0,2},{1,3},{2,0},{3,1},{4,6},{5,7},{6,4},{7,5},{8,10},{9,11},{10,... | collective-permute-start | bytes 98312 | tf_op jit(solution)/shard_map/ppermute | solution.py:295
  8.9 2.8 %collective-permute-start.5 = (bf16[32,512]{1,0:T(8,128)(2,1)S(1)}, bf16[32,512]{1,0:T(8,128)(2,1)S(1)}, u32[]{:S(2)}, u32[]{:S(2)}) collective-permute-start(bf16[32,512]{1,0:T(8,128)(2,1)S(1)} %reshape.20.tokens_ref), channel_id=1, source_target_pairs={{0,1},{1,2},{2,3},{3,0},{4,5},{5,6},{6,7},{7,4},{8,9},{9,10},{10,1... | collective-permute-start | bytes 98312 | tf_op jit(solution)/shard_map/ppermute | solution.py:295
  11.7 1.6 %collective-permute-start.2 = (bf16[32,512]{1,0:T(8,128)(2,1)S(1)}, bf16[32,512]{1,0:T(8,128)(2,1)S(1)}, u32[]{:S(2)}, u32[]{:S(2)}) collective-permute-start(bf16[32,512]{1,0:T(8,128)(2,1)S(1)} %reshape.20.tokens_ref), channel_id=1, source_target_pairs={{0,64},{1,65},{2,66},{3,67},{4,68},{5,69},{6,70},{7,71},{8,72},{9,... | collective-permute-start | bytes 98312 | tf_op jit(solution)/shard_map/ppermute | solution.py:295
  13.3 0.9 %collective-permute-start.1 = (bf16[32,512]{1,0:T(8,128)(2,1)S(1)}, bf16[32,512]{1,0:T(8,128)(2,1)S(1)}, u32[]{:S(2)}, u32[]{:S(2)}) collective-permute-start(bf16[32,512]{1,0:T(8,128)(2,1)S(1)} %reshape.20.tokens_ref), channel_id=1, source_target_pairs={{0,128},{1,129},{2,130},{3,131},{4,132},{5,133},{6,134},{7,135},{8... | collective-permute-start | bytes 98312 | tf_op jit(solution)/shard_map/ppermute | solution.py:295
  15.0 1.1 %fusion.4 = (bf16[128,2,128]{2,1,0:T(2,128)(2,1)S(1)}, bf16[128,2,128]{2,1,0:T(2,128)(2,1)S(1)}) fusion(bf16[128,64,128]{2,1,0:T(8,128)(2,1)} %fine_ref.3), kind=kLoop, calls=%fused_computation.21 | loop fusion | bytes 262144 | tf_op jit(solution)/shard_map/slice | solution.py:320
  16.2 2.5 %collective-permute-start = (bf16[32,512]{1,0:T(8,128)(2,1)S(1)}, bf16[32,512]{1,0:T(8,128)(2,1)S(1)}, u32[]{:S(2)}, u32[]{:S(2)}) collective-permute-start(bf16[32,512]{1,0:T(8,128)(2,1)S(1)} %reshape.20.tokens_ref), channel_id=1, source_target_pairs={{0,192},{1,193},{2,194},{3,195},{4,196},{5,197},{6,198},{7,199},{8... | collective-permute-start | bytes 98312 | tf_op jit(solution)/shard_map/ppermute | solution.py:295
  19.3 2.4 %collective-permute-start.9 = (bf16[128,512]{1,0:T(8,128)(2,1)S(1)}, bf16[128,512]{1,0:T(8,128)(2,1)S(1)}, u32[]{:S(2)}, u32[]{:S(2)}) collective-permute-start(bf16[128,512]{1,0:T(8,128)(2,1)S(1)} %constant_dynamic-update-slice_fusion.5.k0_ref), channel_id=1, source_target_pairs={{0,8},{1,9},{2,10},{3,11},{4,12},{5,13},{6,14},{7,15},{8,0},{9,1},... | collective-permute-start | bytes 393224 | tf_op jit(solution)/shard_map/ppermute | solution.py:295
  21.8 1.8 %collective-permute-start.8 = (bf16[128,512]{1,0:T(8,128)(2,1)S(1)}, bf16[128,512]{1,0:T(8,128)(2,1)S(1)}, u32[]{:S(2)}, u32[]{:S(2)}) collective-permute-start(bf16[128,512]{1,0:T(8,128)(2,1)S(1)} %constant_dynamic-update-slice_fusion.5.k0_ref), channel_id=1, source_target_pairs={{0,4},{1,5},{2,6},{3,7},{4,8},{5,9},{6,10},{7,11},{8,12},{9,13},{1... | collective-permute-start | bytes 393224 | tf_op jit(solution)/shard_map/ppermute | solution.py:295
  23.6 1.1 %collective-permute-start.3 = (bf16[128,512]{1,0:T(8,128)(2,1)S(1)}, bf16[128,512]{1,0:T(8,128)(2,1)S(1)}, u32[]{:S(2)}, u32[]{:S(2)}) collective-permute-start(bf16[128,512]{1,0:T(8,128)(2,1)S(1)} %pad_maximum_fusion.1), channel_id=1, source_target_pairs={{0,32},{1,33},{2,34},{3,35},{4,36},{5,37},{6,38},{7,39},{8,40},{9,... | collective-permute-start | bytes 393224 | tf_op jit(solution)/shard_map/ppermute | solution.py:295
  24.7 4.0 %collective-permute-done.3 = bf16[128,512]{1,0:T(8,128)(2,1)S(1)} collective-permute-done((bf16[128,512]{1,0:T(8,128)(2,1)S(1)}, bf16[128,512]{1,0:T(8,128)(2,1)S(1)}, u32[]{:S(2)}, u32[]{:S(2)}) %collective-permute-start.3) | collective-permute-done | bytes 131104 | tf_op jit(solution)/shard_map/ppermute | solution.py:295
  30.6 1.0 %copy-done.4 = bf16[512,512]{1,0:T(8,128)(2,1)S(1)} copy-done((bf16[512,512]{1,0:T(8,128)(2,1)S(1)}, bf16[512,512]{1,0:T(8,128)(2,1)}, u32[]{:S(2)}) %copy-start.4) | copy-done | bytes 524312
  32.3 5.7 %attention.1 = (f32[256,640]{1,0:T(8,128)S(1)}, bf16[256,640]{1,0:T(8,128)(2,1)S(1)}) custom-call(bf16[256,512]{1,0:T(8,128)(2,1)S(1)} %constant_dynamic-update-slice_fusion.q0_ref, bf16[256,512]{1,0:T(8,128)(2,1)S(1)} %collective-permute-done.4.q1_ref, bf16[128,512]{1,0:T(8,128)(2,1)S(1)} %constant_dynamic-update-slice_fusion.5.k0_ref, ...), custom_call_target="tpu_custom_call" | custom-call | tf_op jit(solution)/shard_map/attention/pallas_call | solution.py:199
  38.8 1.2 %collective-permute-done.11.got_ref = bf16[256,640]{1,0:T(8,128)(2,1)S(1)} collective-permute-done((bf16[256,640]{1,0:T(8,128)(2,1)S(1)}, bf16[256,640]{1,0:T(8,128)(2,1)S(1)}, u32[]{:S(2)}, u32[]{:S(2)}) %collective-permute-start.11) | collective-permute-done | bytes 327712 | tf_op jit(solution)/shard_map/ppermute | solution.py:295
  41.1 4.6 %collective-permute-start.19 = (bf16[132,2,128]{2,1,0:T(2,128)(2,1)S(1)}, bf16[132,2,128]{2,1,0:T(2,128)(2,1)S(1)}, u32[]{:S(2)}, u32[]{:S(2)}) collective-permute-start(bf16[132,2,128]{2,1,0:T(2,128)(2,1)S(1)} %pad_maximum_fusion.3), channel_id=1, source_target_pairs={{0,1},{1,2},{2,3},{3,4},{4,5},{5,6},{6,7},{7,8},{8,9},{9,10},{10,1... | collective-permute-start | bytes 202760 | tf_op jit(solution)/shard_map/ppermute | solution.py:322
  45.8 4.3 %collective-permute-start.18 = (bf16[132,2,128]{2,1,0:T(2,128)(2,1)S(1)}, bf16[132,2,128]{2,1,0:T(2,128)(2,1)S(1)}, u32[]{:S(2)}, u32[]{:S(2)}) collective-permute-start(bf16[132,2,128]{2,1,0:T(2,128)(2,1)S(1)} %pad_maximum_fusion.2), channel_id=1, source_target_pairs={{1,0},{2,1},{3,2},{4,3},{5,4},{6,5},{7,6},{8,7},{9,8},{10,9},{11,1... | collective-permute-start | bytes 202760 | tf_op jit(solution)/shard_map/ppermute | solution.py:323
  50.3 1.8 %collective-permute-start.15 = (bf16[32,640]{1,0:T(8,128)(2,1)S(1)}, bf16[32,640]{1,0:T(8,128)(2,1)S(1)}, u32[]{:S(2)}, u32[]{:S(2)}) collective-permute-start(bf16[32,640]{1,0:T(8,128)(2,1)S(1)} %get-tuple-element.18), channel_id=1, source_target_pairs={{0,192},{1,193},{2,194},{3,195},{4,196},{5,197},{6,198},{7,199},{8... | collective-permute-start | bytes 122888 | tf_op jit(solution)/shard_map/ppermute | solution.py:295
  52.1 1.5 %collective-permute-start.14 = (bf16[32,640]{1,0:T(8,128)(2,1)S(1)}, bf16[32,640]{1,0:T(8,128)(2,1)S(1)}, u32[]{:S(2)}, u32[]{:S(2)}) collective-permute-start(bf16[32,640]{1,0:T(8,128)(2,1)S(1)} %get-tuple-element.19), channel_id=1, source_target_pairs={{0,128},{1,129},{2,130},{3,131},{4,132},{5,133},{6,134},{7,135},{8... | collective-permute-start | bytes 122888 | tf_op jit(solution)/shard_map/ppermute | solution.py:295
  53.6 2.5 %collective-permute-start.13 = (bf16[32,640]{1,0:T(8,128)(2,1)S(1)}, bf16[32,640]{1,0:T(8,128)(2,1)S(1)}, u32[]{:S(2)}, u32[]{:S(2)}) collective-permute-start(bf16[32,640]{1,0:T(8,128)(2,1)S(1)} %get-tuple-element.20), channel_id=1, source_target_pairs={{0,64},{1,65},{2,66},{3,67},{4,68},{5,69},{6,70},{7,71},{8,72},{9,... | collective-permute-start | bytes 122888 | tf_op jit(solution)/shard_map/ppermute | solution.py:295
  56.3 7.3 %first_conv.2.refs_0_ = bf16[35,2,72,128]{3,2,1,0:T(8,128)(2,1)S(1)} custom-call(bf16[128,64,128]{2,1,0:T(8,128)(2,1)S(1)} %copy-done, bf16[2,64,128]{2,1,0:T(8,128)(2,1)S(1)} %collective-permute-done.16.low_ref, bf16[2,64,128]{2,1,0:T(8,128)(2,1)S(1)} %collective-permute-done.17.high_ref, bf16[132,8,128]{2,1,0:T(8,128)(2,1)S(1)} %pad_maximum_fusion.rim_ref, ...), custom_call_target="tpu_custom_call" | custom-call | tf_op jit(solution)/shard_map/first_conv/pallas_call | solution.py:97
  63.6 2.9 %second_conv.2 = f32[32,2,64,128]{3,2,1,0:T(8,128)S(1)} custom-call(bf16[35,2,72,128]{3,2,1,0:T(8,128)(2,1)S(1)} %first_conv.2.refs_0_, bf16[2,3,3,128,128]{4,3,2,1,0:T(8,128)(2,1)S(1)} %copy-done.1, bf16[64,2,64,128]{3,2,1,0:T(8,128)(2,1)S(1)} %bitcast.4), custom_call_target="tpu_custom_call" | custom-call | tf_op jit(solution)/shard_map/second_conv/pallas_call | solution.py:136
  66.6 6.3 %first_conv.3.refs_1_ = bf16[30,2,72,128]{3,2,1,0:T(8,128)(2,1)S(1)} custom-call(bf16[128,64,128]{2,1,0:T(8,128)(2,1)S(1)} %copy-done, bf16[2,64,128]{2,1,0:T(8,128)(2,1)S(1)} %collective-permute-done.16.low_ref, bf16[2,64,128]{2,1,0:T(8,128)(2,1)S(1)} %collective-permute-done.17.high_ref, bf16[132,8,128]{2,1,0:T(8,128)(2,1)S(1)} %pad_maximum_fusion.rim_ref, ...), custom_call_target="tpu_custom_call" | custom-call | tf_op jit(solution)/shard_map/first_conv/pallas_call | solution.py:97
  72.9 3.1 %second_conv.3 = f32[32,2,64,128]{3,2,1,0:T(8,128)S(1)} custom-call(bf16[35,2,72,128]{3,2,1,0:T(8,128)(2,1)S(1)} %first_conv.2.refs_0_, bf16[30,2,72,128]{3,2,1,0:T(8,128)(2,1)S(1)} %first_conv.3.refs_1_, bf16[2,3,3,128,128]{4,3,2,1,0:T(8,128)(2,1)S(1)} %copy-done.1, bf16[64,2,64,128]{3,2,1,0:T(8,128)(2,1)S(1)} %bitcast.5), custom_call_target="tpu_custom_call" | custom-call | tf_op jit(solution)/shard_map/second_conv/pallas_call | solution.py:136
  76.1 2.5 %final.1 = (bf16[128,64,128]{2,1,0:T(8,128)(2,1)}, bf16[8,4,512]{2,1,0:T(4,128)(2,1)}) custom-call(f32[32,640]{1,0:T(8,128)S(1)} %get-tuple-element.12.keep_ref, bf16[32,640]{1,0:T(8,128)(2,1)S(1)} %collective-permute-done.13.g1_ref, bf16[32,640]{1,0:T(8,128)(2,1)S(1)} %collective-permute-done.14.g2_ref, bf16[32,640]{1,0:T(8,128)(2,1)S(1)} %collective-permute-done.15.g3_ref, ...), custom_call_target="tpu_custom_call" | custom-call | tf_op jit(solution)/shard_map/final/pallas_call | solution.py:266
  (64 shorter events, 7.2 us)
Async XLA Ops:
  0.6 29.9 %copy-start.2 = (bf16[512,1024]{1,0:T(8,128)(2,1)S(1)}, bf16[512,1024]{1,0:T(8,128)(2,1)}, u32[]{:S(2)}) copy-start(bf16[512,1024]{1,0:T(8,128)(2,1)} %wkv_ref.1) | copy-start | bytes 3145732
  1.5 17.2 %collective-permute-start.7 = (bf16[32,512]{1,0:T(8,128)(2,1)S(1)}, bf16[32,512]{1,0:T(8,128)(2,1)S(1)}, u32[]{:S(2)}, u32[]{:S(2)}) collective-permute-start(bf16[32,512]{1,0:T(8,128)(2,1)S(1)} %reshape.20.tokens_ref), channel_id=1, source_target_pairs={{0,3},{1,0},{2,1},{3,2},{4,7},{5,4},{6,5},{7,6},{8,11},{9,8},{10,9... | collective-permute-start | bytes 98312 | tf_op jit(solution)/shard_map/ppermute | solution.py:295
  7.9 10.8 %collective-permute-start.6 = (bf16[32,512]{1,0:T(8,128)(2,1)S(1)}, bf16[32,512]{1,0:T(8,128)(2,1)S(1)}, u32[]{:S(2)}, u32[]{:S(2)}) collective-permute-start(bf16[32,512]{1,0:T(8,128)(2,1)S(1)} %reshape.20.tokens_ref), channel_id=1, source_target_pairs={{0,2},{1,3},{2,0},{3,1},{4,6},{5,7},{6,4},{7,5},{8,10},{9,11},{10,... | collective-permute-start | bytes 98312 | tf_op jit(solution)/shard_map/ppermute | solution.py:295
  8.9 7.3 %collective-permute-start.5 = (bf16[32,512]{1,0:T(8,128)(2,1)S(1)}, bf16[32,512]{1,0:T(8,128)(2,1)S(1)}, u32[]{:S(2)}, u32[]{:S(2)}) collective-permute-start(bf16[32,512]{1,0:T(8,128)(2,1)S(1)} %reshape.20.tokens_ref), channel_id=1, source_target_pairs={{0,1},{1,2},{2,3},{3,0},{4,5},{5,6},{6,7},{7,4},{8,9},{9,10},{10,1... | collective-permute-start | bytes 98312 | tf_op jit(solution)/shard_map/ppermute | solution.py:295
  11.7 7.6 %collective-permute-start.2 = (bf16[32,512]{1,0:T(8,128)(2,1)S(1)}, bf16[32,512]{1,0:T(8,128)(2,1)S(1)}, u32[]{:S(2)}, u32[]{:S(2)}) collective-permute-start(bf16[32,512]{1,0:T(8,128)(2,1)S(1)} %reshape.20.tokens_ref), channel_id=1, source_target_pairs={{0,64},{1,65},{2,66},{3,67},{4,68},{5,69},{6,70},{7,71},{8,72},{9,... | collective-permute-start | bytes 98312 | tf_op jit(solution)/shard_map/ppermute | solution.py:295
  13.3 8.5 %collective-permute-start.1 = (bf16[32,512]{1,0:T(8,128)(2,1)S(1)}, bf16[32,512]{1,0:T(8,128)(2,1)S(1)}, u32[]{:S(2)}, u32[]{:S(2)}) collective-permute-start(bf16[32,512]{1,0:T(8,128)(2,1)S(1)} %reshape.20.tokens_ref), channel_id=1, source_target_pairs={{0,128},{1,129},{2,130},{3,131},{4,132},{5,133},{6,134},{7,135},{8... | collective-permute-start | bytes 98312 | tf_op jit(solution)/shard_map/ppermute | solution.py:295
  16.2 7.4 %collective-permute-start = (bf16[32,512]{1,0:T(8,128)(2,1)S(1)}, bf16[32,512]{1,0:T(8,128)(2,1)S(1)}, u32[]{:S(2)}, u32[]{:S(2)}) collective-permute-start(bf16[32,512]{1,0:T(8,128)(2,1)S(1)} %reshape.20.tokens_ref), channel_id=1, source_target_pairs={{0,192},{1,193},{2,194},{3,195},{4,196},{5,197},{6,198},{7,199},{8... | collective-permute-start | bytes 98312 | tf_op jit(solution)/shard_map/ppermute | solution.py:295
  18.7 20.1 %collective-permute-start.17 = (bf16[2,64,128]{2,1,0:T(8,128)(2,1)S(1)}, bf16[2,64,128]{2,1,0:T(8,128)(2,1)S(1)}, u32[]{:S(2)}, u32[]{:S(2)}) collective-permute-start(bf16[2,64,128]{2,1,0:T(8,128)(2,1)S(1)} %get-tuple-element.16), channel_id=1, source_target_pairs={{16,0},{32,16},{48,32},{64,48},{80,64},{96,80},{112,96},{128,112},... | collective-permute-start | bytes 98312 | tf_op jit(solution)/shard_map/ppermute | solution.py:317
  18.7 11.1 %collective-permute-start.10 = (bf16[128,512]{1,0:T(8,128)(2,1)S(1)}, bf16[128,512]{1,0:T(8,128)(2,1)S(1)}, u32[]{:S(2)}, u32[]{:S(2)}) collective-permute-start(bf16[128,512]{1,0:T(8,128)(2,1)S(1)} %constant_dynamic-update-slice_fusion.5.k0_ref), channel_id=1, source_target_pairs={{0,12},{1,13},{2,14},{3,15},{4,0},{5,1},{6,2},{7,3},{8,4},{9,5},{1... | collective-permute-start | bytes 393224 | tf_op jit(solution)/shard_map/ppermute | solution.py:295
  19.3 11.2 %collective-permute-start.9 = (bf16[128,512]{1,0:T(8,128)(2,1)S(1)}, bf16[128,512]{1,0:T(8,128)(2,1)S(1)}, u32[]{:S(2)}, u32[]{:S(2)}) collective-permute-start(bf16[128,512]{1,0:T(8,128)(2,1)S(1)} %constant_dynamic-update-slice_fusion.5.k0_ref), channel_id=1, source_target_pairs={{0,8},{1,9},{2,10},{3,11},{4,12},{5,13},{6,14},{7,15},{8,0},{9,1},... | collective-permute-start | bytes 393224 | tf_op jit(solution)/shard_map/ppermute | solution.py:295
  21.8 8.8 %collective-permute-start.8 = (bf16[128,512]{1,0:T(8,128)(2,1)S(1)}, bf16[128,512]{1,0:T(8,128)(2,1)S(1)}, u32[]{:S(2)}, u32[]{:S(2)}) collective-permute-start(bf16[128,512]{1,0:T(8,128)(2,1)S(1)} %constant_dynamic-update-slice_fusion.5.k0_ref), channel_id=1, source_target_pairs={{0,4},{1,5},{2,6},{3,7},{4,8},{5,9},{6,10},{7,11},{8,12},{9,13},{1... | collective-permute-start | bytes 393224 | tf_op jit(solution)/shard_map/ppermute | solution.py:295
  23.6 5.1 %collective-permute-start.3 = (bf16[128,512]{1,0:T(8,128)(2,1)S(1)}, bf16[128,512]{1,0:T(8,128)(2,1)S(1)}, u32[]{:S(2)}, u32[]{:S(2)}) collective-permute-start(bf16[128,512]{1,0:T(8,128)(2,1)S(1)} %pad_maximum_fusion.1), channel_id=1, source_target_pairs={{0,32},{1,33},{2,34},{3,35},{4,36},{5,37},{6,38},{7,39},{8,40},{9,... | collective-permute-start | bytes 393224 | tf_op jit(solution)/shard_map/ppermute | solution.py:295
  28.7 1.8 %collective-permute-start.4 = (bf16[256,512]{1,0:T(8,128)(2,1)S(1)}, bf16[256,512]{1,0:T(8,128)(2,1)S(1)}, u32[]{:S(2)}, u32[]{:S(2)}) collective-permute-start(bf16[256,512]{1,0:T(8,128)(2,1)S(1)} %constant_dynamic-update-slice_fusion.q0_ref), channel_id=1, source_target_pairs={{0,16},{1,17},{2,18},{3,19},{4,20},{5,21},{6,22},{7,23},{8,24},{9,... | collective-permute-start | bytes 786440 | tf_op jit(solution)/shard_map/ppermute | solution.py:295
  29.8 8.9 %collective-permute-start.16 = (bf16[2,64,128]{2,1,0:T(8,128)(2,1)S(1)}, bf16[2,64,128]{2,1,0:T(8,128)(2,1)S(1)}, u32[]{:S(2)}, u32[]{:S(2)}) collective-permute-start(bf16[2,64,128]{2,1,0:T(8,128)(2,1)S(1)} %get-tuple-element.17), channel_id=1, source_target_pairs={{0,16},{16,32},{32,48},{48,64},{64,80},{80,96},{96,112},{112,128},... | collective-permute-start | bytes 98312 | tf_op jit(solution)/shard_map/ppermute | solution.py:316
  32.3 24.0 %copy-start = (bf16[128,64,128]{2,1,0:T(8,128)(2,1)S(1)}, bf16[128,64,128]{2,1,0:T(8,128)(2,1)}, u32[]{:S(2)}) copy-start(bf16[128,64,128]{2,1,0:T(8,128)(2,1)} %fine_ref.3) | copy-start | bytes 6291460
  32.3 24.0 %copy-start.1 = (bf16[2,3,3,128,128]{4,3,2,1,0:T(8,128)(2,1)S(1)}, bf16[2,3,3,128,128]{4,3,2,1,0:T(8,128)(2,1)}, u32[]{:S(2)}) copy-start(bf16[2,3,3,128,128]{4,3,2,1,0:T(8,128)(2,1)} %refs_2_.1) | copy-start | bytes 1769476
  32.3 24.0 %copy-start.6 = (f32[2,128]{1,0:T(2,128)S(1)}, f32[2,128]{1,0:T(2,128)}, u32[]{:S(2)}) copy-start(f32[2,128]{1,0:T(2,128)} %gains_ref.3) | copy-start | bytes 3076
  38.0 2.0 %collective-permute-start.11 = (bf16[256,640]{1,0:T(8,128)(2,1)S(1)}, bf16[256,640]{1,0:T(8,128)(2,1)S(1)}, u32[]{:S(2)}, u32[]{:S(2)}) collective-permute-start(bf16[256,640]{1,0:T(8,128)(2,1)S(1)} %get-tuple-element.9), channel_id=1, source_target_pairs={{0,16},{1,17},{2,18},{3,19},{4,20},{5,21},{6,22},{7,23},{8,24},{9,... | collective-permute-start | bytes 983048 | tf_op jit(solution)/shard_map/ppermute | solution.py:295
  40.2 9.9 %collective-permute-start.12 = (bf16[128,640]{1,0:T(8,128)(2,1)S(1)}, bf16[128,640]{1,0:T(8,128)(2,1)S(1)}, u32[]{:S(2)}, u32[]{:S(2)}) collective-permute-start(bf16[128,640]{1,0:T(8,128)(2,1)S(1)} %get-tuple-element.11), channel_id=1, source_target_pairs={{0,32},{1,33},{2,34},{3,35},{4,36},{5,37},{6,38},{7,39},{8,40},{9,... | collective-permute-start | bytes 491528 | tf_op jit(solution)/shard_map/ppermute | solution.py:295
  41.1 15.0 %collective-permute-start.19 = (bf16[132,2,128]{2,1,0:T(2,128)(2,1)S(1)}, bf16[132,2,128]{2,1,0:T(2,128)(2,1)S(1)}, u32[]{:S(2)}, u32[]{:S(2)}) collective-permute-start(bf16[132,2,128]{2,1,0:T(2,128)(2,1)S(1)} %pad_maximum_fusion.3), channel_id=1, source_target_pairs={{0,1},{1,2},{2,3},{3,4},{4,5},{5,6},{6,7},{7,8},{8,9},{9,10},{10,1... | collective-permute-start | bytes 202760 | tf_op jit(solution)/shard_map/ppermute | solution.py:322
  45.8 10.3 %collective-permute-start.18 = (bf16[132,2,128]{2,1,0:T(2,128)(2,1)S(1)}, bf16[132,2,128]{2,1,0:T(2,128)(2,1)S(1)}, u32[]{:S(2)}, u32[]{:S(2)}) collective-permute-start(bf16[132,2,128]{2,1,0:T(2,128)(2,1)S(1)} %pad_maximum_fusion.2), channel_id=1, source_target_pairs={{1,0},{2,1},{3,2},{4,3},{5,4},{6,5},{7,6},{8,7},{9,8},{10,9},{11,1... | collective-permute-start | bytes 202760 | tf_op jit(solution)/shard_map/ppermute | solution.py:323
  50.3 25.8 %collective-permute-start.15 = (bf16[32,640]{1,0:T(8,128)(2,1)S(1)}, bf16[32,640]{1,0:T(8,128)(2,1)S(1)}, u32[]{:S(2)}, u32[]{:S(2)}) collective-permute-start(bf16[32,640]{1,0:T(8,128)(2,1)S(1)} %get-tuple-element.18), channel_id=1, source_target_pairs={{0,192},{1,193},{2,194},{3,195},{4,196},{5,197},{6,198},{7,199},{8... | collective-permute-start | bytes 122888 | tf_op jit(solution)/shard_map/ppermute | solution.py:295
  52.1 24.0 %collective-permute-start.14 = (bf16[32,640]{1,0:T(8,128)(2,1)S(1)}, bf16[32,640]{1,0:T(8,128)(2,1)S(1)}, u32[]{:S(2)}, u32[]{:S(2)}) collective-permute-start(bf16[32,640]{1,0:T(8,128)(2,1)S(1)} %get-tuple-element.19), channel_id=1, source_target_pairs={{0,128},{1,129},{2,130},{3,131},{4,132},{5,133},{6,134},{7,135},{8... | collective-permute-start | bytes 122888 | tf_op jit(solution)/shard_map/ppermute | solution.py:295
  53.6 22.5 %collective-permute-start.13 = (bf16[32,640]{1,0:T(8,128)(2,1)S(1)}, bf16[32,640]{1,0:T(8,128)(2,1)S(1)}, u32[]{:S(2)}, u32[]{:S(2)}) collective-permute-start(bf16[32,640]{1,0:T(8,128)(2,1)S(1)} %get-tuple-element.20), channel_id=1, source_target_pairs={{0,64},{1,65},{2,66},{3,67},{4,68},{5,69},{6,70},{7,71},{8,72},{9,... | collective-permute-start | bytes 122888 | tf_op jit(solution)/shard_map/ppermute | solution.py:295
  (4 other events, 8.2 us)

commit v2 on v1

v2 whole, which is shorter than its diff:
```python
import functools
import math
import jax
import jax.numpy as jnp
from jax import lax
from jax.experimental import pallas as pl
from jax.experimental.pallas import tpu as pltpu

from jax.sharding import PartitionSpec as P


WIDE = 80
CIRCLE = 72
SHIFT_BLOCK = 5
F32 = jnp.float32
BF16 = jnp.bfloat16


def unit_rows(v, gain):
    return v * lax.rsqrt(jnp.mean(v * v, axis=-1, keepdims=True) + 1e-06) * gain


def pair_weights(taps_ref, pair_ref):
    zero = jnp.zeros((128, 128), BF16)
    for row in range(4):
        for b in range(3):
            at = (row * 3 + b) * 128
            pair_ref[at : at + 128, 0:128] = taps_ref[row, b] if row < 3 else zero
            pair_ref[at : at + 128, 128:256] = taps_ref[row - 1, b] if row > 0 else zero


def activate_rows(v, half_gain):
    half = v * (lax.rsqrt(jnp.mean(v * v, axis=-1, keepdims=True) + 1e-06) * half_gain)
    return half + half * jnp.tanh(half)


def store_shifted(hidden_ref, p, count, half, value, width):
    at = pl.ds(p, count)
    hidden_ref[0, at, half, :width] = pltpu.roll(value, 1, 1)[:, :width].astype(BF16)
    hidden_ref[1, at, half, :width] = value[:, :width].astype(BF16)
    hidden_ref[2, at, half, :width] = pltpu.roll(value, CIRCLE - 1, 1)[:, :width].astype(BF16)


def conv_pairs(hidden_ref, pair_ref, first, count, width):
    pieces = []
    for row in range(4):
        for b in range(3):
            at = first + row // 2
            piece = hidden_ref[b, at : at + count, row % 2]
            pieces.append(piece.reshape(count * width, 128))
    return jnp.dot(
        jnp.concatenate(pieces, axis=1), pair_ref[...], preferred_element_type=F32
    )


def first_conv_kernel(begin, count, fine_ref, low_ref, high_ref, rim_ref, taps_ref, gains_ref, inside_ref, out_ref, hidden_ref, pair_ref, *own):
    lower, upper = max(begin, 1), min(begin + count + 1, 65)
    block = next(n for n in (5, 7) if (upper - lower) % n == 0)
    bounds = list(range(lower, upper + 1, block))
    copies, rows_ref, first_row = [], fine_ref, 2
    taps, gains = taps_ref.at[0], gains_ref
    if own:
        rows_ref, taps, gains, sems = own
        first_row = 2 * lower
        gain_copy = pltpu.make_async_copy(gains_ref, gains, sems.at[0])
        gain_copy.start()
        for k in range(len(bounds) - 1):
            size = 2 * (bounds[k + 1] - bounds[k])
            copy = pltpu.make_async_copy(
                fine_ref.at[pl.ds(2 * bounds[k] - 2, size)],
                rows_ref.at[pl.ds(2 * (bounds[k] - lower), size)],
                sems.at[2 + k],
            )
            copy.start()
            copies.append(copy)
        taps_copy = pltpu.make_async_copy(taps_ref.at[0], taps, sems.at[1])
        taps_copy.start()
        gain_copy.wait()
    half_gain = 0.5 * gains[0:1, :].reshape(1, 1, 128)

    def activate(main, rim, p, count):
        row = jnp.concatenate([main.astype(F32), rim.astype(F32)], axis=1)
        row = activate_rows(row, half_gain).reshape(count, 2, CIRCLE, 128)
        for half in range(2):
            store_shifted(hidden_ref, p - begin, count, half, row[:, half], CIRCLE)

    if begin == 0:
        activate(low_ref[...], rim_ref[0:2], 0, 1)
    if begin + count == 65:
        activate(high_ref[...], rim_ref[130:132], 65, 1)
    for k, p in enumerate(bounds[:-1]):
        if own:
            copies[k].wait()
        at = 2 * p - first_row
        activate(rows_ref[at : at + 2 * block], rim_ref[2 * p : 2 * p + 2 * block], p, block)
    if own:
        taps_copy.wait()
    pair_weights(taps, pair_ref)
    second_half_gain = 0.5 * gains[1:2, :].reshape(1, 1, 128)
    inside = inside_ref[...].reshape(1, CIRCLE, 128)
    for first in range(0, count, 5):
        both = conv_pairs(hidden_ref, pair_ref, first, 5, WIDE)
        for half in range(2):
            value = both[:, 128 * half : 128 * half + 128].reshape(5, WIDE, 128)[:, :CIRCLE]
            value = activate_rows(value, second_half_gain) * inside
            out_ref[first : first + 5, half] = value.astype(BF16)


VMEM_SPEC = pl.BlockSpec(memory_space=pltpu.VMEM)
ANY_SPEC = pl.BlockSpec(memory_space=pl.ANY)


def first_conv(begin, count, fine, low, high, rim, kernels, gains, inside):
    lower, upper = max(begin, 1), min(begin + count + 1, 65)
    place, scratch = VMEM_SPEC, []
    if begin == 0:
        place = ANY_SPEC
        scratch = [
            pltpu.VMEM((2 * (upper - lower), 64, 128), BF16),
            pltpu.VMEM((3, 3, 128, 128), BF16),
            pltpu.VMEM((2, 128), F32),
            pltpu.SemaphoreType.DMA((2 + 5,)),
        ]
    return pl.pallas_call(
        functools.partial(first_conv_kernel, begin, count),
        out_shape=jax.ShapeDtypeStruct((count, 2, CIRCLE, 128), BF16),
        in_specs=[place, VMEM_SPEC, VMEM_SPEC, VMEM_SPEC, place, place, VMEM_SPEC],
        out_specs=VMEM_SPEC,
        scratch_shapes=[
            pltpu.VMEM((3, count + 1, 2, WIDE, 128), BF16),
            pltpu.VMEM((1536, 256), BF16),
        ] + scratch,
        compiler_params=pltpu.CompilerParams(vmem_limit_bytes=12 << 20),
        name="first_conv",
    )(fine, low, high, rim, kernels, gains, inside)


def second_conv_kernel(begin, pairs, starts, *refs):
    hidden_refs, (taps_ref, fine_ref, out_ref, hidden_ref, pair_ref) = refs[:-5], refs[-5:]
    pair_weights(taps_ref.at[1], pair_ref)
    for ref, start in zip(hidden_refs, starts):
        lower, upper = max(start, begin), min(start + ref.shape[0], begin + pairs + 1)
        for p in range(lower, upper, SHIFT_BLOCK):
            count = min(SHIFT_BLOCK, upper - p)
            for half in range(2):
                value = ref[p - start : p - start + count, half].astype(F32)
                store_shifted(hidden_ref, p - begin, count, half, value, 64)

    for first in range(0, pairs, 8):
        both = conv_pairs(hidden_ref, pair_ref, first, 8, 64)
        for half in range(2):
            value = both[:, 128 * half : 128 * half + 128].reshape(8, 64, 128)
            out_ref[first : first + 8, half] = value + fine_ref[begin + first : begin + first + 8, half].astype(F32)


def second_conv(begin, pairs, starts, hidden, kernels, fine):
    return pl.pallas_call(
        functools.partial(second_conv_kernel, begin, pairs, starts),
        out_shape=jax.ShapeDtypeStruct((pairs, 2, 64, 128), F32),
        in_specs=[VMEM_SPEC] * (len(hidden) + 2),
        out_specs=VMEM_SPEC,
        scratch_shapes=[pltpu.VMEM((3, pairs + 1, 2, 64, 128), BF16), pltpu.VMEM((1536, 256), BF16)],
        compiler_params=pltpu.CompilerParams(vmem_limit_bytes=12 << 20),
        name="second_conv",
    )(*hidden, kernels, fine.reshape(64, 2, 64, 128))


def high_low(v):
    high = v.astype(BF16)
    return high, (v - high.astype(F32)).astype(BF16)


def split_blocks(value, keep_ref, send_ref, columns):
    for i in range(value.shape[0] // 64):
        keep_ref[32 * i : 32 * i + 32, columns] = value[64 * i : 64 * i + 32]
        send_ref[32 * i : 32 * i + 32, columns] = value[64 * i + 32 : 64 * i + 64].astype(BF16)


def attention_kernel(q0_ref, q1_ref, k0_ref, k1_ref, gain_ref, head_ref, wq_ref, wkv_ref, keep_ref, send_ref):
    gain = gain_ref[...]
    lane = lax.broadcasted_iota(jnp.int32, (1, 128), 1)
    even = lane < 64

    def head_norm(v, head_gain):
        square = v * v
        sums = [jnp.sum(jnp.where(own, square, 0.0), axis=-1, keepdims=True) for own in (even, jnp.logical_not(even))]
        mean = jnp.where(even, sums[0], sums[1]) * (1.0 / 64)
        return v * lax.rsqrt(mean + 1e-06) * head_gain

    query_rows = jnp.concatenate([q0_ref[...], q1_ref[...]], axis=0).astype(F32)
    query_rows = unit_rows(query_rows, gain).astype(BF16)
    key_rows = jnp.concatenate([k0_ref[...], k1_ref[...]], axis=0).astype(F32)
    key_rows = unit_rows(key_rows, gain).astype(BF16)
    scale = 1.0 / math.sqrt(64)
    totals = jnp.zeros((512, 128), F32)
    queries = jnp.dot(query_rows, wq_ref[...], preferred_element_type=F32)
    keys = jnp.dot(key_rows, wkv_ref[:, :512], preferred_element_type=F32)
    values = jnp.dot(key_rows, wkv_ref[:, 512:], preferred_element_type=F32)
    for g in range(4):
        at = 128 * g
        q = queries[:, at : at + 128]
        q = (head_norm(q, head_ref[0:1, :]) * scale).astype(BF16)
        k = keys[:, at : at + 128]
        k = head_norm(k, head_ref[1:2, :])
        v = values[:, at : at + 128]
        parts = []
        for side in range(2):
            own = even if side == 0 else jnp.logical_not(even)
            k_own = jnp.where(own, k, 0.0).astype(BF16)
            v_own = jnp.where(own, v, 1.0).astype(BF16)
            scores = lax.dot_general(q, k_own, (((1,), (1,)), ((), ())), preferred_element_type=F32)
            weights = jnp.exp(scores).astype(BF16)
            parts.append(jnp.dot(weights, v_own, preferred_element_type=F32))
        summed = jnp.where(even, parts[0], parts[1])
        total = jnp.where(even, parts[1], parts[0])
        high = total.astype(BF16).astype(F32)
        totals = totals + jnp.where(lane % 64 == 2 * g, high, jnp.where(lane % 64 == 2 * g + 1, total - high, 0.0))
        split_blocks(summed, keep_ref, send_ref, slice(at, at + 128))
    split_blocks(totals, keep_ref, send_ref, slice(512, 640))


def attention(q0, q1, ks, token_gain, head_gains, wq, wkv):
    head2 = jnp.concatenate([head_gains, head_gains], axis=1)
    return pl.pallas_call(
        attention_kernel,
        out_shape=(jax.ShapeDtypeStruct((256, 640), F32), jax.ShapeDtypeStruct((256, 640), BF16)),
        in_specs=[VMEM_SPEC] * 8,
        out_specs=(VMEM_SPEC, VMEM_SPEC),
        compiler_params=pltpu.CompilerParams(vmem_limit_bytes=16 << 20),
        name="attention",
    )(q0, q1, *ks, token_gain.reshape(1, 512), head2, wq, wkv)


def split_totals(x):
    lane = lax.broadcasted_iota(jnp.int32, (1, 128), 1)
    total = x + pltpu.roll(x, 127, 1)
    high = total.astype(BF16).astype(F32)
    return jnp.where(lane % 2 == 0, high, pltpu.roll(total - high, 1, 1))


def reduce_kernel(keep_ref, got_ref, out_ref, send_ref):
    total = keep_ref[...] + got_ref[...].astype(F32)
    if out_ref.shape[0] == send_ref.shape[0]:
        split_blocks(total[:, :512], out_ref, send_ref, slice(0, 512))
        even_out = [total[64 * i : 64 * i + 32, 512:] for i in range(total.shape[0] // 64)]
        odd_out = [total[64 * i + 32 : 64 * i + 64, 512:] for i in range(total.shape[0] // 64)]
        out_ref[:, 512:] = jnp.concatenate(even_out, axis=0)
        send_ref[:, 512:] = split_totals(jnp.concatenate(odd_out, axis=0)).astype(BF16)
    else:
        rows = out_ref.shape[0]
        out_ref[...] = total[:rows]
        send_ref[:, :512] = total[rows:, :512].astype(BF16)
        send_ref[:, 512:] = split_totals(total[rows:, 512:]).astype(BF16)


def reduce_step(keep, got, rows):
    count = keep.shape[0]
    return pl.pallas_call(
        reduce_kernel,
        out_shape=(jax.ShapeDtypeStruct((rows, 640), F32), jax.ShapeDtypeStruct((count - rows, 640), BF16)),
        in_specs=[VMEM_SPEC] * 2,
        out_specs=(VMEM_SPEC, VMEM_SPEC),
        compiler_params=pltpu.CompilerParams(vmem_limit_bytes=4 << 20),
        name="reduce_step",
    )(keep, got)


def final_kernel(keep_ref, g1_ref, g2_ref, g3_ref, tokens_ref, wo_ref, we_ref, s0_ref, s1_ref, out_ref, coarse_ref, lifted_ref, block_ref, sems):
    total = keep_ref[...] + g1_ref[...].astype(F32) + g2_ref[...].astype(F32) + g3_ref[...].astype(F32)
    r = lax.broadcasted_iota(jnp.int32, (128, 512), 0)
    head = lax.broadcasted_iota(jnp.int32, (128, 512), 1) // 64
    at = jnp.where(head % 2 == 1, 0, 64) + head // 2 * 2
    pick = jnp.where((r == at) | (r == at + 1), 1.0, 0.0).astype(BF16)
    high, low = high_low(total[:, 512:])
    spread = jnp.dot(high, pick, preferred_element_type=F32) + jnp.dot(low, pick, preferred_element_type=F32)
    attended = (total[:, :512] / spread).astype(BF16)
    coarse = tokens_ref[...].astype(F32) + jnp.dot(attended, wo_ref[...], preferred_element_type=F32)
    rounded = coarse.astype(BF16)
    lifted_ref[...] = jnp.dot(rounded, we_ref[...], preferred_element_type=F32)
    for a in range(8):
        coarse_ref[a] = coarse[4 * a : 4 * a + 4].astype(BF16)
    copies = []
    for a in range(8):
        for b in range(4):
            row = lifted_ref[4 * a + b : 4 * a + b + 1, :].reshape(1, 1, 128)
            cols = slice(16 * b, 16 * b + 16)
            half_ref, at = (s0_ref, 16 * a) if a < 4 else (s1_ref, 16 * a - 64)
            block_ref[a, :, cols] = (half_ref[at : at + 16, cols] + row).astype(BF16)
        copy = pltpu.make_async_copy(block_ref.at[a], out_ref.at[pl.ds(16 * a, 16)], sems.at[a])
        copy.start()
        copies.append(copy)
    for copy in copies:
        copy.wait()


def final(keep, got, tokens, wo, we, second):
    return pl.pallas_call(
        final_kernel,
        out_shape=(jax.ShapeDtypeStruct((128, 64, 128), BF16), jax.ShapeDtypeStruct((8, 4, 512), BF16)),
        in_specs=[VMEM_SPEC] * 9,
        out_specs=(ANY_SPEC, VMEM_SPEC),
        scratch_shapes=[pltpu.VMEM((32, 128), F32), pltpu.VMEM((8, 16, 64, 128), BF16), pltpu.SemaphoreType.DMA((8,))],
        compiler_params=pltpu.CompilerParams(vmem_limit_bytes=12 << 20),
        name="final",
    )(keep, *got, tokens, wo, we, *second)


AXES = ("lon", "lat")


def device_pairs(move):
    pairs = []
    for y in range(4):
        for zl in range(2):
            for c in range(2):
                for x in range(4):
                    for zh in range(4):
                        ty, tl, tc, tx, th = move(y, zl, c, x, zh)
                        source = ((y * 2 + zl) * 2 + c) * 16 + x * 4 + zh
                        target = ((ty * 2 + tl) * 2 + tc) * 16 + tx * 4 + th
                        pairs.append((source, target))
    return pairs


def move(value, y=0, low=0, core=0, x=0, high=0):
    return lax.ppermute(
        value, AXES,
        device_pairs(lambda a, b, c, d, e: (a ^ y, b ^ low, c ^ core, d ^ x, e ^ high)),
    )


def block(
    fine_state,
    coarse_state,
    norm_gains,
    kernels,
    token_gain,
    head_gains,
    query_weight,
    keyvalue_weight,
    output_weight,
    expand_weight,
):
    count = 16
    place = lax.axis_index("lon"), lax.axis_index("lat")
    even = [at % 2 == 0 for at in place]
    inner = [(i, i ^ 1) for i in range(count)]
    outer = [(i, (i + 1) % count if i % 2 else (i - 1) % count) for i in range(count)]
    top, bottom = fine_state[:2], fine_state[-2:]
    got_inner = lax.ppermute(jnp.where(even[0], bottom, top), "lon", inner)
    got_outer = lax.ppermute(jnp.where(even[0], top, bottom), "lon", outer)
    low = jnp.where(even[0], got_outer, got_inner)
    high = jnp.where(even[0], got_inner, got_outer)
    tokens = coarse_state.reshape(32, 512)
    near = jnp.concatenate([tokens, move(tokens, core=1)], axis=0)
    far = jnp.concatenate([tokens, move(tokens, high=1)], axis=0)
    first = jnp.concatenate([low[:, :2], fine_state[:, :2], high[:, :2]], axis=0)
    last = jnp.concatenate([low[:, -2:], fine_state[:, -2:], high[:, -2:]], axis=0)
    got_inner = lax.ppermute(jnp.where(even[1], last, first), "lat", inner)
    got_outer = lax.ppermute(jnp.where(even[1], first, last), "lat", outer[1:-1])
    left = jnp.where(even[1], got_outer, got_inner)
    right = jnp.where(even[1], got_inner, got_outer)
    near = jnp.concatenate([near, move(near, low=1)], axis=0)
    far = jnp.concatenate([far, move(far, high=2)], axis=0)
    rim = jnp.concatenate([right, jnp.zeros((132, 4, 128), BF16), left], axis=1)
    position = lax.broadcasted_iota(jnp.int32, (CIRCLE, 128), 0)
    column = place[1] * 64 + jnp.where(position < 68, position, position - CIRCLE)
    inside = jnp.where((column >= 0) & (column < 64 * count), 1.0, 0.0).astype(F32)
    hidden = []
    starts = (0, 25, 45, 65)

    def conv(k):
        hidden.append(
            first_conv(starts[k], starts[k + 1] - starts[k], fine_state, low, high, rim, kernels, norm_gains, inside)
        )

    conv(0)
    near = jnp.concatenate([near, move(near, y=1)], axis=0)
    far = jnp.concatenate([far, move(far, x=1)], axis=0)
    conv(1)
    across = move(near, y=2)
    key_tokens = [far, move(far, x=2)]
    conv(2)
    keep, out = attention(near, across, key_tokens, token_gain, head_gains, query_weight, keyvalue_weight)
    keep, out = reduce_step(keep, move(out, core=1), 128)
    got = move(out, low=1)
    second_a = second_conv(0, 32, starts[:2], hidden[:2], kernels, fine_state)
    keep, out = reduce_step(keep, got, 32)
    got = [move(out[32 * k - 32 : 32 * k], y=k) for k in (1, 2, 3)]
    second_b = second_conv(32, 32, starts[1:3], hidden[1:], kernels, fine_state)
    second = [half.reshape(64, 64, 128) for half in (second_a, second_b)]
    return final(keep, got, tokens, output_weight, expand_weight, second)


def solution(mesh):
    return jax.shard_map(
        block,
        mesh=mesh,
        in_specs=(
            P("lon", "lat", None),
            P("lon", "lat", None),
            P(),
            P(),
            P(),
            P(),
            P(),
            P(),
            P(),
            P(),
        ),
        out_specs=(P("lon", "lat", None), P("lon", "lat", None)),
        check_vma=False,
    )
```

time: 79.1 us -> 77.1 us (0.975)
  the two profiles are of different devices: /device:TPU:10 before, /device:TPU:6 now
where the time goes in v2:
time: 77.1 us; the launch traced here: 76.9 us
  starting transfers between devices  31.3 us (41%)
  waiting for transfers between devices  20.8 us (27%)
  Pallas kernels  19.2 us (25%)
  local copies, waits for them, and re-layouts  2.23 us (3%)
  other arithmetic  2.17 us (3%)
  between operations  1.11 us (1%)
    ppermute x13, starting transfers between devices, move(): lax.ppermute(value, AXES, device_pairs(lambda a, b, c, d, e: (a ^ y, b ^...  21.7 us
    ppermute x13, waiting for transfers between devices, move(): lax.ppermute(value, AXES, device_pairs(lambda a, b, c, d, e: (a ^ y, b ^...  18.2 us
    pallas_call x3, Pallas kernels, first_conv(): pl.pallas_call(functools.partial(first_conv_kernel, begin, count), out_sh...  8.96 us
    ppermute x1, starting transfers between devices, block(): lax.ppermute(jnp.where(even[1], first, last), 'lat', outer[1:-1])  4.15 us
    ppermute x1, starting transfers between devices, block(): got_outer = lax.ppermute(jnp.where(even[0], top, bottom), 'lon', outer)  4.07 us
    pallas_call x2, Pallas kernels, second_conv(): pl.pallas_call(functools.partial(second_conv_kernel, begin, pairs, starts...  3.96 us
    pallas_call x1, Pallas kernels, attention(): pl.pallas_call(attention_kernel, out_shape=(jax.ShapeDtypeStruct((256, 64...  3.49 us
    ppermute x1, waiting for transfers between devices, block(): lax.ppermute(jnp.where(even[1], first, last), 'lat', outer[1:-1])  2.56 us
  transfers between devices with their start and end apart: 17, of which 6 were waited for; matrix products, arithmetic and copies ran while one was open for 4% of the time, Pallas kernels for 17%

profile of v2, /device:TPU:6, one launch (start us, length us, event | category | flops | bytes accessed | tf_op | source)
XLA Modules:
  0.0 76.9 jit_solution(6857210534550618054)
XLA Ops:
  1.5 3.4 %collective-permute-start.4 = (bf16[32,512]{1,0:T(8,128)(2,1)S(1)}, bf16[32,512]{1,0:T(8,128)(2,1)S(1)}, u32[]{:S(2)}, u32[]{:S(2)}) collective-permute-start(bf16[32,512]{1,0:T(8,128)(2,1)S(1)} %reshape.20.tokens_ref), channel_id=1, source_target_pairs={{0,1},{1,0},{2,3},{3,2},{4,5},{5,4},{6,7},{7,6},{8,9},{9,8},{10,11... | collective-permute-start | bytes 98312 | tf_op jit(solution)/shard_map/ppermute | solution.py:326
  6.3 4.1 %collective-permute-start.13 = (bf16[2,64,128]{2,1,0:T(8,128)(2,1)S(1)}, bf16[2,64,128]{2,1,0:T(8,128)(2,1)S(1)}, u32[]{:S(2)}, u32[]{:S(2)}) collective-permute-start(bf16[2,64,128]{2,1,0:T(8,128)(2,1)S(1)} %get-tuple-element.17), channel_id=1, source_target_pairs={{0,240},{16,32},{32,16},{48,64},{64,48},{80,96},{96,80},{112,128},... | collective-permute-start | bytes 98312 | tf_op jit(solution)/shard_map/ppermute | solution.py:351
  10.4 1.1 %fusion.6 = (bf16[128,2,128]{2,1,0:T(2,128)(2,1)S(1)}, bf16[128,2,128]{2,1,0:T(2,128)(2,1)S(1)}) fusion(bf16[128,64,128]{2,1,0:T(8,128)(2,1)} %fine_ref.5), kind=kLoop, calls=%fused_computation.33 | loop fusion | bytes 262144 | tf_op jit(solution)/shard_map/slice | solution.py:358
  12.4 4.6 %collective-permute-start.5 = (bf16[64,512]{1,0:T(8,128)(2,1)S(1)}, bf16[64,512]{1,0:T(8,128)(2,1)S(1)}, u32[]{:S(2)}, u32[]{:S(2)}) collective-permute-start(bf16[64,512]{1,0:T(8,128)(2,1)S(1)} %get-tuple-element.33), channel_id=1, source_target_pairs={{0,2},{1,3},{2,0},{3,1},{4,6},{5,7},{6,4},{7,5},{8,10},{9,11},{10,... | collective-permute-start | bytes 196616 | tf_op jit(solution)/shard_map/ppermute | solution.py:326
  17.0 4.4 %collective-permute-done.5 = bf16[64,512]{1,0:T(8,128)(2,1)S(1)} collective-permute-done((bf16[64,512]{1,0:T(8,128)(2,1)S(1)}, bf16[64,512]{1,0:T(8,128)(2,1)S(1)}, u32[]{:S(2)}, u32[]{:S(2)}) %collective-permute-start.5) | collective-permute-done | bytes 65568 | tf_op jit(solution)/shard_map/ppermute | solution.py:326
  22.3 1.0 %collective-permute-start.2 = (bf16[128,512]{1,0:T(8,128)(2,1)S(1)}, bf16[128,512]{1,0:T(8,128)(2,1)S(1)}, u32[]{:S(2)}, u32[]{:S(2)}) collective-permute-start(bf16[128,512]{1,0:T(8,128)(2,1)S(1)} %get-tuple-element.32), channel_id=1, source_target_pairs={{0,64},{1,65},{2,66},{3,67},{4,68},{5,69},{6,70},{7,71},{8,72},{9,... | collective-permute-start | bytes 393224 | tf_op jit(solution)/shard_map/ppermute | solution.py:326
  23.4 3.9 %collective-permute-done.2 = bf16[128,512]{1,0:T(8,128)(2,1)S(1)} collective-permute-done((bf16[128,512]{1,0:T(8,128)(2,1)S(1)}, bf16[128,512]{1,0:T(8,128)(2,1)S(1)}, u32[]{:S(2)}, u32[]{:S(2)}) %collective-permute-start.2) | collective-permute-done | bytes 131104 | tf_op jit(solution)/shard_map/ppermute | solution.py:326
  27.3 3.3 %collective-permute-start.3 = (bf16[256,512]{1,0:T(8,128)(2,1)S(1)}, bf16[256,512]{1,0:T(8,128)(2,1)S(1)}, u32[]{:S(2)}, u32[]{:S(2)}) collective-permute-start(bf16[256,512]{1,0:T(8,128)(2,1)S(1)} %constant_dynamic-update-slice_fusion.q0_ref), channel_id=1, source_target_pairs={{0,128},{1,129},{2,130},{3,131},{4,132},{5,133},{6,134},{7,135},{8... | collective-permute-start | bytes 786440 | tf_op jit(solution)/shard_map/ppermute | solution.py:326
  30.6 1.2 %collective-permute-start.7 = (bf16[256,512]{1,0:T(8,128)(2,1)S(1)}, bf16[256,512]{1,0:T(8,128)(2,1)S(1)}, u32[]{:S(2)}, u32[]{:S(2)}) collective-permute-start(bf16[256,512]{1,0:T(8,128)(2,1)S(1)} %constant_dynamic-update-slice_fusion.4.k0_ref), channel_id=1, source_target_pairs={{0,8},{1,9},{2,10},{3,11},{4,12},{5,13},{6,14},{7,15},{8,0},{9,1},... | collective-permute-start | bytes 786440 | tf_op jit(solution)/shard_map/ppermute | solution.py:326
  31.9 4.2 %collective-permute-done.3.q1_ref = bf16[256,512]{1,0:T(8,128)(2,1)S(1)} collective-permute-done((bf16[256,512]{1,0:T(8,128)(2,1)S(1)}, bf16[256,512]{1,0:T(8,128)(2,1)S(1)}, u32[]{:S(2)}, u32[]{:S(2)}) %collective-permute-start.3) | collective-permute-done | bytes 262176 | tf_op jit(solution)/shard_map/ppermute | solution.py:326
  36.1 3.1 %collective-permute-done.7.k1_ref = bf16[256,512]{1,0:T(8,128)(2,1)S(1)} collective-permute-done((bf16[256,512]{1,0:T(8,128)(2,1)S(1)}, bf16[256,512]{1,0:T(8,128)(2,1)S(1)}, u32[]{:S(2)}, u32[]{:S(2)}) %collective-permute-start.7) | collective-permute-done | bytes 262176 | tf_op jit(solution)/shard_map/ppermute | solution.py:326
  39.2 3.5 %attention.1 = (f32[256,640]{1,0:T(8,128)S(1)}, bf16[256,640]{1,0:T(8,128)(2,1)S(1)}) custom-call(bf16[256,512]{1,0:T(8,128)(2,1)S(1)} %constant_dynamic-update-slice_fusion.q0_ref, bf16[256,512]{1,0:T(8,128)(2,1)S(1)} %collective-permute-done.3.q1_ref, bf16[256,512]{1,0:T(8,128)(2,1)S(1)} %constant_dynamic-update-slice_fusion.4.k0_ref, ...), custom_call_target="tpu_custom_call" | custom-call | tf_op jit(solution)/shard_map/attention/pallas_call | solution.py:224
  43.8 4.2 %collective-permute-start.16 = (bf16[132,2,128]{2,1,0:T(2,128)(2,1)S(1)}, bf16[132,2,128]{2,1,0:T(2,128)(2,1)S(1)}, u32[]{:S(2)}, u32[]{:S(2)}) collective-permute-start(bf16[132,2,128]{2,1,0:T(2,128)(2,1)S(1)} %get-tuple-element.21), channel_id=1, source_target_pairs={{1,2},{2,1},{3,4},{4,3},{5,6},{6,5},{7,8},{8,7},{9,10},{10,9},{11,... | collective-permute-start | bytes 202760 | tf_op jit(solution)/shard_map/ppermute | solution.py:360
  48.3 2.9 %collective-permute-start.9 = (bf16[128,640]{1,0:T(8,128)(2,1)S(1)}, bf16[128,640]{1,0:T(8,128)(2,1)S(1)}, u32[]{:S(2)}, u32[]{:S(2)}) collective-permute-start(bf16[128,640]{1,0:T(8,128)(2,1)S(1)} %get-tuple-element.11), channel_id=1, source_target_pairs={{0,32},{1,33},{2,34},{3,35},{4,36},{5,37},{6,38},{7,39},{8,40},{9,... | collective-permute-start | bytes 491528 | tf_op jit(solution)/shard_map/ppermute | solution.py:326
  51.2 2.6 %collective-permute-done.16 = bf16[132,2,128]{2,1,0:T(2,128)(2,1)S(1)} collective-permute-done((bf16[132,2,128]{2,1,0:T(2,128)(2,1)S(1)}, bf16[132,2,128]{2,1,0:T(2,128)(2,1)S(1)}, u32[]{:S(2)}, u32[]{:S(2)}) %collective-permute-start.16) | collective-permute-done | bytes 67616 | tf_op jit(solution)/shard_map/ppermute | solution.py:360
  53.8 2.7 %collective-permute-done.9.got_ref = bf16[128,640]{1,0:T(8,128)(2,1)S(1)} collective-permute-done((bf16[128,640]{1,0:T(8,128)(2,1)S(1)}, bf16[128,640]{1,0:T(8,128)(2,1)S(1)}, u32[]{:S(2)}, u32[]{:S(2)}) %collective-permute-start.9) | collective-permute-done | bytes 163872 | tf_op jit(solution)/shard_map/ppermute | solution.py:326
  56.6 1.6 %collective-permute-start.12 = (bf16[32,640]{1,0:T(8,128)(2,1)S(1)}, bf16[32,640]{1,0:T(8,128)(2,1)S(1)}, u32[]{:S(2)}, u32[]{:S(2)}) collective-permute-start(bf16[32,640]{1,0:T(8,128)(2,1)S(1)} %get-tuple-element.22), channel_id=1, source_target_pairs={{0,192},{1,193},{2,194},{3,195},{4,196},{5,197},{6,198},{7,199},{8... | collective-permute-start | bytes 122888 | tf_op jit(solution)/shard_map/ppermute | solution.py:326
  59.1 1.9 %collective-permute-start.10 = (bf16[32,640]{1,0:T(8,128)(2,1)S(1)}, bf16[32,640]{1,0:T(8,128)(2,1)S(1)}, u32[]{:S(2)}, u32[]{:S(2)}) collective-permute-start(bf16[32,640]{1,0:T(8,128)(2,1)S(1)} %get-tuple-element.24), channel_id=1, source_target_pairs={{0,64},{1,65},{2,66},{3,67},{4,68},{5,69},{6,70},{7,71},{8,72},{9,... | collective-permute-start | bytes 122888 | tf_op jit(solution)/shard_map/ppermute | solution.py:326
  61.2 2.1 %first_conv.4.refs_1_.refs_0_ = bf16[20,2,72,128]{3,2,1,0:T(8,128)(2,1)S(1)} custom-call(bf16[128,64,128]{2,1,0:T(8,128)(2,1)S(1)} %copy-done, bf16[2,64,128]{2,1,0:T(8,128)(2,1)S(1)} %get-tuple-element.26.low_ref, bf16[2,64,128]{2,1,0:T(8,128)(2,1)S(1)} %get-tuple-element.25.high_ref, bf16[132,8,128]{2,1,0:T(8,128)(2,1)S(1)} %pad_maximum_fusion.rim_ref, ...), custom_call_target="tpu_custom_call" | custom-call | tf_op jit(solution)/shard_map/first_conv/pallas_call | solution.py:124
  63.3 2.1 %first_conv.5.refs_1_ = bf16[20,2,72,128]{3,2,1,0:T(8,128)(2,1)S(1)} custom-call(bf16[128,64,128]{2,1,0:T(8,128)(2,1)S(1)} %copy-done, bf16[2,64,128]{2,1,0:T(8,128)(2,1)S(1)} %get-tuple-element.26.low_ref, bf16[2,64,128]{2,1,0:T(8,128)(2,1)S(1)} %get-tuple-element.25.high_ref, bf16[132,8,128]{2,1,0:T(8,128)(2,1)S(1)} %pad_maximum_fusion.rim_ref, ...), custom_call_target="tpu_custom_call" | custom-call | tf_op jit(solution)/shard_map/first_conv/pallas_call | solution.py:124
  65.5 4.7 %first_conv.3.refs_0_ = bf16[25,2,72,128]{3,2,1,0:T(8,128)(2,1)S(1)} custom-call(bf16[128,64,128]{2,1,0:T(8,128)(2,1)S(1)} %copy-done, bf16[2,64,128]{2,1,0:T(8,128)(2,1)S(1)} %get-tuple-element.26.low_ref, bf16[2,64,128]{2,1,0:T(8,128)(2,1)S(1)} %get-tuple-element.25.high_ref, bf16[132,8,128]{2,1,0:T(8,128)(2,1)S(1)} %pad_maximum_fusion.rim_ref, ...), custom_call_target="tpu_custom_call" | custom-call | tf_op jit(solution)/shard_map/first_conv/pallas_call | solution.py:124
  70.2 2.0 %second_conv.2 = f32[32,2,64,128]{3,2,1,0:T(8,128)S(1)} custom-call(bf16[25,2,72,128]{3,2,1,0:T(8,128)(2,1)S(1)} %first_conv.3.refs_0_, bf16[20,2,72,128]{3,2,1,0:T(8,128)(2,1)S(1)} %first_conv.4.refs_1_.refs_0_, bf16[2,3,3,128,128]{4,3,2,1,0:T(8,128)(2,1)S(1)} %copy-done.1, bf16[64,2,64,128]{3,2,1,0:T(8,128)(2,1)S(1)} %bitcast.8), custom_call_target="tpu_custom_call" | custom-call | tf_op jit(solution)/shard_map/second_conv/pallas_call | solution.py:157
  72.2 2.0 %second_conv.3 = f32[32,2,64,128]{3,2,1,0:T(8,128)S(1)} custom-call(bf16[20,2,72,128]{3,2,1,0:T(8,128)(2,1)S(1)} %first_conv.4.refs_1_.refs_0_, bf16[20,2,72,128]{3,2,1,0:T(8,128)(2,1)S(1)} %first_conv.5.refs_1_, bf16[2,3,3,128,128]{4,3,2,1,0:T(8,128)(2,1)S(1)} %copy-done.1, bf16[64,2,64,128]{3,2,1,0:T(8,128)(2,1)S(1)} %bitcast.9), custom_call_target="tpu_custom_call" | custom-call | tf_op jit(solution)/shard_map/second_conv/pallas_call | solution.py:157
  74.2 2.5 %final.1 = (bf16[128,64,128]{2,1,0:T(8,128)(2,1)}, bf16[8,4,512]{2,1,0:T(4,128)(2,1)}) custom-call(f32[32,640]{1,0:T(8,128)S(1)} %get-tuple-element.12.keep_ref, bf16[32,640]{1,0:T(8,128)(2,1)S(1)} %collective-permute-done.10.g1_ref, bf16[32,640]{1,0:T(8,128)(2,1)S(1)} %collective-permute-done.11.g2_ref, bf16[32,640]{1,0:T(8,128)(2,1)S(1)} %collective-permute-done.12.g3_ref, ...), custom_call_target="tpu_custom_call" | custom-call | tf_op jit(solution)/shard_map/final/pallas_call | solution.py:297
  (60 shorter events, 6.9 us)
Async XLA Ops:
  0.6 38.5 %copy-start.2 = (bf16[512,1024]{1,0:T(8,128)(2,1)S(1)}, bf16[512,1024]{1,0:T(8,128)(2,1)}, u32[]{:S(2)}) copy-start(bf16[512,1024]{1,0:T(8,128)(2,1)} %wkv_ref.1) | copy-start | bytes 3145732
  0.6 38.5 %copy-start.4 = (bf16[512,512]{1,0:T(8,128)(2,1)S(1)}, bf16[512,512]{1,0:T(8,128)(2,1)}, u32[]{:S(2)}) copy-start(bf16[512,512]{1,0:T(8,128)(2,1)} %wq_ref.1) | copy-start | bytes 1572868
  0.7 38.5 %copy-start.7 = (f32[512]{0:T(512)S(1)}, f32[512]{0:T(512)}, u32[]{:S(2)}) copy-start(f32[512]{0:T(512)} %param.14) | copy-start | bytes 6148
  1.5 10.8 %collective-permute-start.4 = (bf16[32,512]{1,0:T(8,128)(2,1)S(1)}, bf16[32,512]{1,0:T(8,128)(2,1)S(1)}, u32[]{:S(2)}, u32[]{:S(2)}) collective-permute-start(bf16[32,512]{1,0:T(8,128)(2,1)S(1)} %reshape.20.tokens_ref), channel_id=1, source_target_pairs={{0,1},{1,0},{2,3},{3,2},{4,5},{5,4},{6,7},{7,6},{8,9},{9,8},{10,11... | collective-permute-start | bytes 98312 | tf_op jit(solution)/shard_map/ppermute | solution.py:326
  4.9 7.5 %collective-permute-start = (bf16[32,512]{1,0:T(8,128)(2,1)S(1)}, bf16[32,512]{1,0:T(8,128)(2,1)S(1)}, u32[]{:S(2)}, u32[]{:S(2)}) collective-permute-start(bf16[32,512]{1,0:T(8,128)(2,1)S(1)} %reshape.20.tokens_ref), channel_id=1, source_target_pairs={{0,16},{1,17},{2,18},{3,19},{4,20},{5,21},{6,22},{7,23},{8,24},{9,... | collective-permute-start | bytes 98312 | tf_op jit(solution)/shard_map/ppermute | solution.py:326
  5.7 26.1 %collective-permute-start.14 = (bf16[2,64,128]{2,1,0:T(8,128)(2,1)S(1)}, bf16[2,64,128]{2,1,0:T(8,128)(2,1)S(1)}, u32[]{:S(2)}, u32[]{:S(2)}) collective-permute-start(bf16[2,64,128]{2,1,0:T(8,128)(2,1)S(1)} %get-tuple-element.16), channel_id=1, source_target_pairs={{0,16},{16,0},{32,48},{48,32},{64,80},{80,64},{96,112},{112,96},{1... | collective-permute-start | bytes 98312 | tf_op jit(solution)/shard_map/ppermute | solution.py:350
  6.3 25.6 %collective-permute-start.13 = (bf16[2,64,128]{2,1,0:T(8,128)(2,1)S(1)}, bf16[2,64,128]{2,1,0:T(8,128)(2,1)S(1)}, u32[]{:S(2)}, u32[]{:S(2)}) collective-permute-start(bf16[2,64,128]{2,1,0:T(8,128)(2,1)S(1)} %get-tuple-element.17), channel_id=1, source_target_pairs={{0,240},{16,32},{32,16},{48,64},{64,48},{80,96},{96,80},{112,128},... | collective-permute-start | bytes 98312 | tf_op jit(solution)/shard_map/ppermute | solution.py:351
  12.4 9.0 %collective-permute-start.5 = (bf16[64,512]{1,0:T(8,128)(2,1)S(1)}, bf16[64,512]{1,0:T(8,128)(2,1)S(1)}, u32[]{:S(2)}, u32[]{:S(2)}) collective-permute-start(bf16[64,512]{1,0:T(8,128)(2,1)S(1)} %get-tuple-element.33), channel_id=1, source_target_pairs={{0,2},{1,3},{2,0},{3,1},{4,6},{5,7},{6,4},{7,5},{8,10},{9,11},{10,... | collective-permute-start | bytes 196616 | tf_op jit(solution)/shard_map/ppermute | solution.py:326
  17.0 4.4 %collective-permute-start.1 = (bf16[64,512]{1,0:T(8,128)(2,1)S(1)}, bf16[64,512]{1,0:T(8,128)(2,1)S(1)}, u32[]{:S(2)}, u32[]{:S(2)}) collective-permute-start(bf16[64,512]{1,0:T(8,128)(2,1)S(1)} %get-tuple-element.34), channel_id=1, source_target_pairs={{0,32},{1,33},{2,34},{3,35},{4,36},{5,37},{6,38},{7,39},{8,40},{9,... | collective-permute-start | bytes 196616 | tf_op jit(solution)/shard_map/ppermute | solution.py:326
  21.4 9.2 %collective-permute-start.6 = (bf16[128,512]{1,0:T(8,128)(2,1)S(1)}, bf16[128,512]{1,0:T(8,128)(2,1)S(1)}, u32[]{:S(2)}, u32[]{:S(2)}) collective-permute-start(bf16[128,512]{1,0:T(8,128)(2,1)S(1)} %get-tuple-element.31), channel_id=1, source_target_pairs={{0,4},{1,5},{2,6},{3,7},{4,0},{5,1},{6,2},{7,3},{8,12},{9,13},{10,... | collective-permute-start | bytes 393224 | tf_op jit(solution)/shard_map/ppermute | solution.py:326
  22.3 5.0 %collective-permute-start.2 = (bf16[128,512]{1,0:T(8,128)(2,1)S(1)}, bf16[128,512]{1,0:T(8,128)(2,1)S(1)}, u32[]{:S(2)}, u32[]{:S(2)}) collective-permute-start(bf16[128,512]{1,0:T(8,128)(2,1)S(1)} %get-tuple-element.32), channel_id=1, source_target_pairs={{0,64},{1,65},{2,66},{3,67},{4,68},{5,69},{6,70},{7,71},{8,72},{9,... | collective-permute-start | bytes 393224 | tf_op jit(solution)/shard_map/ppermute | solution.py:326
  27.3 8.8 %collective-permute-start.3 = (bf16[256,512]{1,0:T(8,128)(2,1)S(1)}, bf16[256,512]{1,0:T(8,128)(2,1)S(1)}, u32[]{:S(2)}, u32[]{:S(2)}) collective-permute-start(bf16[256,512]{1,0:T(8,128)(2,1)S(1)} %constant_dynamic-update-slice_fusion.q0_ref), channel_id=1, source_target_pairs={{0,128},{1,129},{2,130},{3,131},{4,132},{5,133},{6,134},{7,135},{8... | collective-permute-start | bytes 786440 | tf_op jit(solution)/shard_map/ppermute | solution.py:326
  30.6 8.5 %collective-permute-start.7 = (bf16[256,512]{1,0:T(8,128)(2,1)S(1)}, bf16[256,512]{1,0:T(8,128)(2,1)S(1)}, u32[]{:S(2)}, u32[]{:S(2)}) collective-permute-start(bf16[256,512]{1,0:T(8,128)(2,1)S(1)} %constant_dynamic-update-slice_fusion.4.k0_ref), channel_id=1, source_target_pairs={{0,8},{1,9},{2,10},{3,11},{4,12},{5,13},{6,14},{7,15},{8,0},{9,1},... | collective-permute-start | bytes 786440 | tf_op jit(solution)/shard_map/ppermute | solution.py:326
  39.1 22.0 %copy-start = (bf16[128,64,128]{2,1,0:T(8,128)(2,1)S(1)}, bf16[128,64,128]{2,1,0:T(8,128)(2,1)}, u32[]{:S(2)}) copy-start(bf16[128,64,128]{2,1,0:T(8,128)(2,1)} %fine_ref.5) | copy-start | bytes 6291460
  39.2 22.0 %copy-start.1 = (bf16[2,3,3,128,128]{4,3,2,1,0:T(8,128)(2,1)S(1)}, bf16[2,3,3,128,128]{4,3,2,1,0:T(8,128)(2,1)}, u32[]{:S(2)}) copy-start(bf16[2,3,3,128,128]{4,3,2,1,0:T(8,128)(2,1)} %refs_2_.3) | copy-start | bytes 1769476
  39.2 22.0 %copy-start.6 = (f32[2,128]{1,0:T(2,128)S(1)}, f32[2,128]{1,0:T(2,128)}, u32[]{:S(2)}) copy-start(f32[2,128]{1,0:T(2,128)} %gains_ref.5) | copy-start | bytes 3076
  42.7 5.5 %collective-permute-start.8 = (bf16[256,640]{1,0:T(8,128)(2,1)S(1)}, bf16[256,640]{1,0:T(8,128)(2,1)S(1)}, u32[]{:S(2)}, u32[]{:S(2)}) collective-permute-start(bf16[256,640]{1,0:T(8,128)(2,1)S(1)} %get-tuple-element.9), channel_id=1, source_target_pairs={{0,16},{1,17},{2,18},{3,19},{4,20},{5,21},{6,22},{7,23},{8,24},{9,... | collective-permute-start | bytes 983048 | tf_op jit(solution)/shard_map/ppermute | solution.py:326
  43.0 8.2 %collective-permute-start.15 = (bf16[132,2,128]{2,1,0:T(2,128)(2,1)S(1)}, bf16[132,2,128]{2,1,0:T(2,128)(2,1)S(1)}, u32[]{:S(2)}, u32[]{:S(2)}) collective-permute-start(bf16[132,2,128]{2,1,0:T(2,128)(2,1)S(1)} %get-tuple-element.20), channel_id=1, source_target_pairs={{0,1},{1,0},{2,3},{3,2},{4,5},{5,4},{6,7},{7,6},{8,9},{9,8},{10,11... | collective-permute-start | bytes 202760 | tf_op jit(solution)/shard_map/ppermute | solution.py:359
  43.8 9.9 %collective-permute-start.16 = (bf16[132,2,128]{2,1,0:T(2,128)(2,1)S(1)}, bf16[132,2,128]{2,1,0:T(2,128)(2,1)S(1)}, u32[]{:S(2)}, u32[]{:S(2)}) collective-permute-start(bf16[132,2,128]{2,1,0:T(2,128)(2,1)S(1)} %get-tuple-element.21), channel_id=1, source_target_pairs={{1,2},{2,1},{3,4},{4,3},{5,6},{6,5},{7,8},{8,7},{9,10},{10,9},{11,... | collective-permute-start | bytes 202760 | tf_op jit(solution)/shard_map/ppermute | solution.py:360
  48.3 8.1 %collective-permute-start.9 = (bf16[128,640]{1,0:T(8,128)(2,1)S(1)}, bf16[128,640]{1,0:T(8,128)(2,1)S(1)}, u32[]{:S(2)}, u32[]{:S(2)}) collective-permute-start(bf16[128,640]{1,0:T(8,128)(2,1)S(1)} %get-tuple-element.11), channel_id=1, source_target_pairs={{0,32},{1,33},{2,34},{3,35},{4,36},{5,37},{6,38},{7,39},{8,40},{9,... | collective-permute-start | bytes 491528 | tf_op jit(solution)/shard_map/ppermute | solution.py:326
  56.6 17.5 %collective-permute-start.12 = (bf16[32,640]{1,0:T(8,128)(2,1)S(1)}, bf16[32,640]{1,0:T(8,128)(2,1)S(1)}, u32[]{:S(2)}, u32[]{:S(2)}) collective-permute-start(bf16[32,640]{1,0:T(8,128)(2,1)S(1)} %get-tuple-element.22), channel_id=1, source_target_pairs={{0,192},{1,193},{2,194},{3,195},{4,196},{5,197},{6,198},{7,199},{8... | collective-permute-start | bytes 122888 | tf_op jit(solution)/shard_map/ppermute | solution.py:326
  58.2 16.0 %collective-permute-start.11 = (bf16[32,640]{1,0:T(8,128)(2,1)S(1)}, bf16[32,640]{1,0:T(8,128)(2,1)S(1)}, u32[]{:S(2)}, u32[]{:S(2)}) collective-permute-start(bf16[32,640]{1,0:T(8,128)(2,1)S(1)} %get-tuple-element.23), channel_id=1, source_target_pairs={{0,128},{1,129},{2,130},{3,131},{4,132},{5,133},{6,134},{7,135},{8... | collective-permute-start | bytes 122888 | tf_op jit(solution)/shard_map/ppermute | solution.py:326
  59.1 15.1 %collective-permute-start.10 = (bf16[32,640]{1,0:T(8,128)(2,1)S(1)}, bf16[32,640]{1,0:T(8,128)(2,1)S(1)}, u32[]{:S(2)}, u32[]{:S(2)}) collective-permute-start(bf16[32,640]{1,0:T(8,128)(2,1)S(1)} %get-tuple-element.24), channel_id=1, source_target_pairs={{0,64},{1,65},{2,66},{3,67},{4,68},{5,69},{6,70},{7,71},{8,72},{9,... | collective-permute-start | bytes 122888 | tf_op jit(solution)/shard_map/ppermute | solution.py:326
  72.2 2.0 %copy-start.3 = (bf16[512,512]{1,0:T(8,128)(2,1)S(1)}, bf16[512,512]{1,0:T(8,128)(2,1)}, u32[]{:S(2)}) copy-start(bf16[512,512]{1,0:T(8,128)(2,1)} %wo_ref.1) | copy-start | bytes 1572868
  (1 other events, 2.0 us)

commit v3 on v2

--- a/solution.py
+++ b/solution.py
@@ -53,29 +53,10 @@
     )
 
 
-def first_conv_kernel(begin, count, fine_ref, low_ref, high_ref, rim_ref, taps_ref, gains_ref, inside_ref, out_ref, hidden_ref, pair_ref, *own):
+def first_conv_kernel(begin, count, fine_ref, low_ref, high_ref, rim_ref, taps_ref, gains_ref, inside_ref, out_ref, hidden_ref, pair_ref):
     lower, upper = max(begin, 1), min(begin + count + 1, 65)
     block = next(n for n in (5, 7) if (upper - lower) % n == 0)
-    bounds = list(range(lower, upper + 1, block))
-    copies, rows_ref, first_row = [], fine_ref, 2
     taps, gains = taps_ref.at[0], gains_ref
-    if own:
-        rows_ref, taps, gains, sems = own
-        first_row = 2 * lower
-        gain_copy = pltpu.make_async_copy(gains_ref, gains, sems.at[0])
-        gain_copy.start()
-        for k in range(len(bounds) - 1):
-            size = 2 * (bounds[k + 1] - bounds[k])
-            copy = pltpu.make_async_copy(
-                fine_ref.at[pl.ds(2 * bounds[k] - 2, size)],
-                rows_ref.at[pl.ds(2 * (bounds[k] - lower), size)],
-                sems.at[2 + k],
-            )
-            copy.start()
-            copies.append(copy)
-        taps_copy = pltpu.make_async_copy(taps_ref.at[0], taps, sems.at[1])
-        taps_copy.start()
-        gain_copy.wait()
     half_gain = 0.5 * gains[0:1, :].reshape(1, 1, 128)
 
     def activate(main, rim, p, count):
@@ -88,13 +69,8 @@
         activate(low_ref[...], rim_ref[0:2], 0, 1)
     if begin + count == 65:
         activate(high_ref[...], rim_ref[130:132], 65, 1)
-    for k, p in enumerate(bounds[:-1]):
-        if own:
-            copies[k].wait()
-        at = 2 * p - first_row
-        activate(rows_ref[at : at + 2 * block], rim_ref[2 * p : 2 * p + 2 * block], p, block)
-    if own:
-        taps_copy.wait()
+    for p in range(lower, upper, block):
+        activate(fine_ref[2 * p - 2 : 2 * p - 2 + 2 * block], rim_ref[2 * p : 2 * p + 2 * block], p, block)
     pair_weights(taps, pair_ref)
     second_half_gain = 0.5 * gains[1:2, :].reshape(1, 1, 128)
     inside = inside_ref[...].reshape(1, CIRCLE, 128)
@@ -111,25 +87,15 @@
 
 
 def first_conv(begin, count, fine, low, high, rim, kernels, gains, inside):
-    lower, upper = max(begin, 1), min(begin + count + 1, 65)
-    place, scratch = VMEM_SPEC, []
-    if begin == 0:
-        place = ANY_SPEC
-        scratch = [
-            pltpu.VMEM((2 * (upper - lower), 64, 128), BF16),
-            pltpu.VMEM((3, 3, 128, 128), BF16),
-            pltpu.VMEM((2, 128), F32),
-            pltpu.SemaphoreType.DMA((2 + 5,)),
-        ]
     return pl.pallas_call(
         functools.partial(first_conv_kernel, begin, count),
         out_shape=jax.ShapeDtypeStruct((count, 2, CIRCLE, 128), BF16),
-        in_specs=[place, VMEM_SPEC, VMEM_SPEC, VMEM_SPEC, place, place, VMEM_SPEC],
+        in_specs=[VMEM_SPEC] * 7,
         out_specs=VMEM_SPEC,
         scratch_shapes=[
             pltpu.VMEM((3, count + 1, 2, WIDE, 128), BF16),
             pltpu.VMEM((1536, 256), BF16),
-        ] + scratch,
+        ],
         compiler_params=pltpu.CompilerParams(vmem_limit_bytes=12 << 20),
         name="first_conv",
     )(fine, low, high, rim, kernels, gains, inside)
@@ -361,13 +327,13 @@
     left = jnp.where(even[1], got_outer, got_inner)
     right = jnp.where(even[1], got_inner, got_outer)
     near = jnp.concatenate([near, move(near, low=1)], axis=0)
-    far = jnp.concatenate([far, move(far, high=2)], axis=0)
+    far = jnp.concatenate([far, move(far, high=3)], axis=0)
     rim = jnp.concatenate([right, jnp.zeros((132, 4, 128), BF16), left], axis=1)
     position = lax.broadcasted_iota(jnp.int32, (CIRCLE, 128), 0)
     column = place[1] * 64 + jnp.where(position < 68, position, position - CIRCLE)
     inside = jnp.where((column >= 0) & (column < 64 * count), 1.0, 0.0).astype(F32)
     hidden = []
-    starts = (0, 25, 45, 65)
+    starts = (0, 15, 35, 65)
 
     def conv(k):
         hidden.append(
@@ -378,15 +344,15 @@
     near = jnp.concatenate([near, move(near, y=1)], axis=0)
     far = jnp.concatenate([far, move(far, x=1)], axis=0)
     conv(1)
-    across = move(near, y=2)
-    key_tokens = [far, move(far, x=2)]
+    across = move(near, y=3)
+    key_tokens = [far, move(far, x=3)]
     conv(2)
     keep, out = attention(near, across, key_tokens, token_gain, head_gains, query_weight, keyvalue_weight)
     keep, out = reduce_step(keep, move(out, core=1), 128)
     got = move(out, low=1)
     second_a = second_conv(0, 32, starts[:2], hidden[:2], kernels, fine_state)
     keep, out = reduce_step(keep, got, 32)
-    got = [move(out[32 * k - 32 : 32 * k], y=k) for k in (1, 2, 3)]
+    got = [move(out[32 * i : 32 * i + 32], y=k) for i, k in enumerate((1, 3, 2))]
     second_b = second_conv(32, 32, starts[1:3], hidden[1:], kernels, fine_state)
     second = [half.reshape(64, 64, 128) for half in (second_a, second_b)]
     return final(keep, got, tokens, output_weight, expand_weight, second)

time: 77.1 us -> 71.9 us (0.933)
  the two profiles are of different devices: /device:TPU:6 before, /device:TPU:10 now
where the time goes in v3:
time: 71.9 us; the launch traced here: 71.7 us
  starting transfers between devices  31.6 us (44%)
  waiting for transfers between devices  17.5 us (24%)
  Pallas kernels  17.1 us (24%)
  local copies, waits for them, and re-layouts  2.23 us (3%)
  other arithmetic  2.17 us (3%)
  between operations  1.1 us (2%)
    ppermute x13, starting transfers between devices, move(): lax.ppermute(value, AXES, device_pairs(lambda a, b, c, d, e: (a ^ y, b ^...  23.8 us
    ppermute x13, waiting for transfers between devices, move(): lax.ppermute(value, AXES, device_pairs(lambda a, b, c, d, e: (a ^ y, b ^...  16.1 us
    pallas_call x3, Pallas kernels, first_conv(): pl.pallas_call(functools.partial(first_conv_kernel, begin, count), out_sh...  6.83 us
    ppermute x1, starting transfers between devices, block(): lax.ppermute(jnp.where(even[1], first, last), 'lat', outer[1:-1])  5.05 us
    pallas_call x2, Pallas kernels, second_conv(): pl.pallas_call(functools.partial(second_conv_kernel, begin, pairs, starts...  3.97 us
    pallas_call x1, Pallas kernels, attention(): pl.pallas_call(attention_kernel, out_shape=(jax.ShapeDtypeStruct((256, 64...  3.49 us
    pallas_call x1, Pallas kernels, final(): pl.pallas_call(final_kernel, out_shape=(jax.ShapeDtypeStruct((128, 64, 12...  2.5 us
    ppermute x1, starting transfers between devices, block(): got_outer = lax.ppermute(jnp.where(even[0], top, bottom), 'lon', outer)  1.51 us
  transfers between devices with their start and end apart: 17, of which 7 were waited for; matrix products, arithmetic and copies ran while one was open for 5% of the time, Pallas kernels for 15%

profile of v3, /device:TPU:10, one launch (start us, length us, event | category | flops | bytes accessed | tf_op | source)
XLA Modules:
  0.0 71.7 jit_solution(4185340641477551683)
XLA Ops:
  1.5 3.4 %collective-permute-start.4 = (bf16[32,512]{1,0:T(8,128)(2,1)S(1)}, bf16[32,512]{1,0:T(8,128)(2,1)S(1)}, u32[]{:S(2)}, u32[]{:S(2)}) collective-permute-start(bf16[32,512]{1,0:T(8,128)(2,1)S(1)} %reshape.20.tokens_ref), channel_id=1, source_target_pairs={{0,1},{1,0},{2,3},{3,2},{4,5},{5,4},{6,7},{7,6},{8,9},{9,8},{10,11... | collective-permute-start | bytes 98312 | tf_op jit(solution)/shard_map/ppermute | solution.py:292
  6.3 1.5 %collective-permute-start.13 = (bf16[2,64,128]{2,1,0:T(8,128)(2,1)S(1)}, bf16[2,64,128]{2,1,0:T(8,128)(2,1)S(1)}, u32[]{:S(2)}, u32[]{:S(2)}) collective-permute-start(bf16[2,64,128]{2,1,0:T(8,128)(2,1)S(1)} %get-tuple-element.17), channel_id=1, source_target_pairs={{0,240},{16,32},{32,16},{48,64},{64,48},{80,96},{96,80},{112,128},... | collective-permute-start | bytes 98312 | tf_op jit(solution)/shard_map/ppermute | solution.py:317
  9.8 3.7 %collective-permute-start.5 = (bf16[64,512]{1,0:T(8,128)(2,1)S(1)}, bf16[64,512]{1,0:T(8,128)(2,1)S(1)}, u32[]{:S(2)}, u32[]{:S(2)}) collective-permute-start(bf16[64,512]{1,0:T(8,128)(2,1)S(1)} %get-tuple-element.33), channel_id=1, source_target_pairs={{0,3},{1,2},{2,1},{3,0},{4,7},{5,6},{6,5},{7,4},{8,11},{9,10},{10,... | collective-permute-start | bytes 196616 | tf_op jit(solution)/shard_map/ppermute | solution.py:292
  14.6 2.1 %collective-permute-done.5 = bf16[64,512]{1,0:T(8,128)(2,1)S(1)} collective-permute-done((bf16[64,512]{1,0:T(8,128)(2,1)S(1)}, bf16[64,512]{1,0:T(8,128)(2,1)S(1)}, u32[]{:S(2)}, u32[]{:S(2)}) %collective-permute-start.5) | collective-permute-done | bytes 65568 | tf_op jit(solution)/shard_map/ppermute | solution.py:292
  16.7 1.8 %collective-permute-done.1 = bf16[64,512]{1,0:T(8,128)(2,1)S(1)} collective-permute-done((bf16[64,512]{1,0:T(8,128)(2,1)S(1)}, bf16[64,512]{1,0:T(8,128)(2,1)S(1)}, u32[]{:S(2)}, u32[]{:S(2)}) %collective-permute-start.1) | collective-permute-done | bytes 65568 | tf_op jit(solution)/shard_map/ppermute | solution.py:292
  19.2 2.2 %collective-permute-start.2 = (bf16[128,512]{1,0:T(8,128)(2,1)S(1)}, bf16[128,512]{1,0:T(8,128)(2,1)S(1)}, u32[]{:S(2)}, u32[]{:S(2)}) collective-permute-start(bf16[128,512]{1,0:T(8,128)(2,1)S(1)} %get-tuple-element.32), channel_id=1, source_target_pairs={{0,64},{1,65},{2,66},{3,67},{4,68},{5,69},{6,70},{7,71},{8,72},{9,... | collective-permute-start | bytes 393224 | tf_op jit(solution)/shard_map/ppermute | solution.py:292
  21.5 3.1 %collective-permute-done.2 = bf16[128,512]{1,0:T(8,128)(2,1)S(1)} collective-permute-done((bf16[128,512]{1,0:T(8,128)(2,1)S(1)}, bf16[128,512]{1,0:T(8,128)(2,1)S(1)}, u32[]{:S(2)}, u32[]{:S(2)}) %collective-permute-start.2) | collective-permute-done | bytes 131104 | tf_op jit(solution)/shard_map/ppermute | solution.py:292
  24.6 1.8 %collective-permute-start.3 = (bf16[256,512]{1,0:T(8,128)(2,1)S(1)}, bf16[256,512]{1,0:T(8,128)(2,1)S(1)}, u32[]{:S(2)}, u32[]{:S(2)}) collective-permute-start(bf16[256,512]{1,0:T(8,128)(2,1)S(1)} %constant_dynamic-update-slice_fusion.q0_ref), channel_id=1, source_target_pairs={{0,192},{1,193},{2,194},{3,195},{4,196},{5,197},{6,198},{7,199},{8... | collective-permute-start | bytes 786440 | tf_op jit(solution)/shard_map/ppermute | solution.py:292
  26.4 2.2 %collective-permute-start.7 = (bf16[256,512]{1,0:T(8,128)(2,1)S(1)}, bf16[256,512]{1,0:T(8,128)(2,1)S(1)}, u32[]{:S(2)}, u32[]{:S(2)}) collective-permute-start(bf16[256,512]{1,0:T(8,128)(2,1)S(1)} %constant_dynamic-update-slice_fusion.4.k0_ref), channel_id=1, source_target_pairs={{0,12},{1,13},{2,14},{3,15},{4,8},{5,9},{6,10},{7,11},{8,4},{9,5},... | collective-permute-start | bytes 786440 | tf_op jit(solution)/shard_map/ppermute | solution.py:292
  28.7 3.2 %collective-permute-done.3.q1_ref = bf16[256,512]{1,0:T(8,128)(2,1)S(1)} collective-permute-done((bf16[256,512]{1,0:T(8,128)(2,1)S(1)}, bf16[256,512]{1,0:T(8,128)(2,1)S(1)}, u32[]{:S(2)}, u32[]{:S(2)}) %collective-permute-start.3) | collective-permute-done | bytes 262176 | tf_op jit(solution)/shard_map/ppermute | solution.py:292
  31.9 2.0 %collective-permute-done.7.k1_ref = bf16[256,512]{1,0:T(8,128)(2,1)S(1)} collective-permute-done((bf16[256,512]{1,0:T(8,128)(2,1)S(1)}, bf16[256,512]{1,0:T(8,128)(2,1)S(1)}, u32[]{:S(2)}, u32[]{:S(2)}) %collective-permute-start.7) | collective-permute-done | bytes 262176 | tf_op jit(solution)/shard_map/ppermute | solution.py:292
  33.9 3.5 %attention.1 = (f32[256,640]{1,0:T(8,128)S(1)}, bf16[256,640]{1,0:T(8,128)(2,1)S(1)}) custom-call(bf16[256,512]{1,0:T(8,128)(2,1)S(1)} %constant_dynamic-update-slice_fusion.q0_ref, bf16[256,512]{1,0:T(8,128)(2,1)S(1)} %collective-permute-done.3.q1_ref, bf16[256,512]{1,0:T(8,128)(2,1)S(1)} %constant_dynamic-update-slice_fusion.4.k0_ref, ...), custom_call_target="tpu_custom_call" | custom-call | tf_op jit(solution)/shard_map/attention/pallas_call | solution.py:190
  38.4 5.0 %collective-permute-start.16 = (bf16[132,2,128]{2,1,0:T(2,128)(2,1)S(1)}, bf16[132,2,128]{2,1,0:T(2,128)(2,1)S(1)}, u32[]{:S(2)}, u32[]{:S(2)}) collective-permute-start(bf16[132,2,128]{2,1,0:T(2,128)(2,1)S(1)} %get-tuple-element.21), channel_id=1, source_target_pairs={{1,2},{2,1},{3,4},{4,3},{5,6},{6,5},{7,8},{8,7},{9,10},{10,9},{11,... | collective-permute-start | bytes 202760 | tf_op jit(solution)/shard_map/ppermute | solution.py:326
  43.8 3.7 %collective-permute-start.9 = (bf16[128,640]{1,0:T(8,128)(2,1)S(1)}, bf16[128,640]{1,0:T(8,128)(2,1)S(1)}, u32[]{:S(2)}, u32[]{:S(2)}) collective-permute-start(bf16[128,640]{1,0:T(8,128)(2,1)S(1)} %get-tuple-element.11), channel_id=1, source_target_pairs={{0,32},{1,33},{2,34},{3,35},{4,36},{5,37},{6,38},{7,39},{8,40},{9,... | collective-permute-start | bytes 491528 | tf_op jit(solution)/shard_map/ppermute | solution.py:292
  47.5 1.3 %collective-permute-done.16 = bf16[132,2,128]{2,1,0:T(2,128)(2,1)S(1)} collective-permute-done((bf16[132,2,128]{2,1,0:T(2,128)(2,1)S(1)}, bf16[132,2,128]{2,1,0:T(2,128)(2,1)S(1)}, u32[]{:S(2)}, u32[]{:S(2)}) %collective-permute-start.16) | collective-permute-done | bytes 67616 | tf_op jit(solution)/shard_map/ppermute | solution.py:326
  48.9 3.9 %collective-permute-done.9.got_ref = bf16[128,640]{1,0:T(8,128)(2,1)S(1)} collective-permute-done((bf16[128,640]{1,0:T(8,128)(2,1)S(1)}, bf16[128,640]{1,0:T(8,128)(2,1)S(1)}, u32[]{:S(2)}, u32[]{:S(2)}) %collective-permute-start.9) | collective-permute-done | bytes 163872 | tf_op jit(solution)/shard_map/ppermute | solution.py:292
  53.0 1.3 %collective-permute-start.12 = (bf16[32,640]{1,0:T(8,128)(2,1)S(1)}, bf16[32,640]{1,0:T(8,128)(2,1)S(1)}, u32[]{:S(2)}, u32[]{:S(2)}) collective-permute-start(bf16[32,640]{1,0:T(8,128)(2,1)S(1)} %get-tuple-element.22), channel_id=1, source_target_pairs={{0,128},{1,129},{2,130},{3,131},{4,132},{5,133},{6,134},{7,135},{8... | collective-permute-start | bytes 122888 | tf_op jit(solution)/shard_map/ppermute | solution.py:292
  55.2 2.7 %collective-permute-start.10 = (bf16[32,640]{1,0:T(8,128)(2,1)S(1)}, bf16[32,640]{1,0:T(8,128)(2,1)S(1)}, u32[]{:S(2)}, u32[]{:S(2)}) collective-permute-start(bf16[32,640]{1,0:T(8,128)(2,1)S(1)} %get-tuple-element.24), channel_id=1, source_target_pairs={{0,64},{1,65},{2,66},{3,67},{4,68},{5,69},{6,70},{7,71},{8,72},{9,... | collective-permute-start | bytes 122888 | tf_op jit(solution)/shard_map/ppermute | solution.py:292
  58.1 1.6 %first_conv.3.refs_0_ = bf16[15,2,72,128]{3,2,1,0:T(8,128)(2,1)S(1)} custom-call(bf16[128,64,128]{2,1,0:T(8,128)(2,1)S(1)} %copy-done, bf16[2,64,128]{2,1,0:T(8,128)(2,1)S(1)} %get-tuple-element.26.low_ref, bf16[2,64,128]{2,1,0:T(8,128)(2,1)S(1)} %get-tuple-element.25.high_ref, bf16[132,8,128]{2,1,0:T(8,128)(2,1)S(1)} %pad_maximum_fusion.rim_ref, ...), custom_call_target="tpu_custom_call" | custom-call | tf_op jit(solution)/shard_map/first_conv/pallas_call | solution.py:90
  59.8 2.1 %first_conv.4.refs_1_.refs_0_ = bf16[20,2,72,128]{3,2,1,0:T(8,128)(2,1)S(1)} custom-call(bf16[128,64,128]{2,1,0:T(8,128)(2,1)S(1)} %copy-done, bf16[2,64,128]{2,1,0:T(8,128)(2,1)S(1)} %get-tuple-element.26.low_ref, bf16[2,64,128]{2,1,0:T(8,128)(2,1)S(1)} %get-tuple-element.25.high_ref, bf16[132,8,128]{2,1,0:T(8,128)(2,1)S(1)} %pad_maximum_fusion.rim_ref, ...), custom_call_target="tpu_custom_call" | custom-call | tf_op jit(solution)/shard_map/first_conv/pallas_call | solution.py:90
  61.9 3.1 %first_conv.5.refs_1_ = bf16[30,2,72,128]{3,2,1,0:T(8,128)(2,1)S(1)} custom-call(bf16[128,64,128]{2,1,0:T(8,128)(2,1)S(1)} %copy-done, bf16[2,64,128]{2,1,0:T(8,128)(2,1)S(1)} %get-tuple-element.26.low_ref, bf16[2,64,128]{2,1,0:T(8,128)(2,1)S(1)} %get-tuple-element.25.high_ref, bf16[132,8,128]{2,1,0:T(8,128)(2,1)S(1)} %pad_maximum_fusion.rim_ref, ...), custom_call_target="tpu_custom_call" | custom-call | tf_op jit(solution)/shard_map/first_conv/pallas_call | solution.py:90
  65.0 2.0 %second_conv.3 = f32[32,2,64,128]{3,2,1,0:T(8,128)S(1)} custom-call(bf16[20,2,72,128]{3,2,1,0:T(8,128)(2,1)S(1)} %first_conv.4.refs_1_.refs_0_, bf16[30,2,72,128]{3,2,1,0:T(8,128)(2,1)S(1)} %first_conv.5.refs_1_, bf16[2,3,3,128,128]{4,3,2,1,0:T(8,128)(2,1)S(1)} %copy-done.1, bf16[64,2,64,128]{3,2,1,0:T(8,128)(2,1)S(1)} %bitcast.8), custom_call_target="tpu_custom_call" | custom-call | tf_op jit(solution)/shard_map/second_conv/pallas_call | solution.py:123
  67.0 2.0 %second_conv.2 = f32[32,2,64,128]{3,2,1,0:T(8,128)S(1)} custom-call(bf16[15,2,72,128]{3,2,1,0:T(8,128)(2,1)S(1)} %first_conv.3.refs_0_, bf16[20,2,72,128]{3,2,1,0:T(8,128)(2,1)S(1)} %first_conv.4.refs_1_.refs_0_, bf16[2,3,3,128,128]{4,3,2,1,0:T(8,128)(2,1)S(1)} %copy-done.1, bf16[64,2,64,128]{3,2,1,0:T(8,128)(2,1)S(1)} %bitcast.9), custom_call_target="tpu_custom_call" | custom-call | tf_op jit(solution)/shard_map/second_conv/pallas_call | solution.py:123
  69.0 2.5 %final.1 = (bf16[128,64,128]{2,1,0:T(8,128)(2,1)}, bf16[8,4,512]{2,1,0:T(4,128)(2,1)}) custom-call(f32[32,640]{1,0:T(8,128)S(1)} %get-tuple-element.12.keep_ref, bf16[32,640]{1,0:T(8,128)(2,1)S(1)} %collective-permute-done.10.g1_ref, bf16[32,640]{1,0:T(8,128)(2,1)S(1)} %collective-permute-done.11.g2_ref, bf16[32,640]{1,0:T(8,128)(2,1)S(1)} %collective-permute-done.12.g3_ref, ...), custom_call_target="tpu_custom_call" | custom-call | tf_op jit(solution)/shard_map/final/pallas_call | solution.py:263
  (60 shorter events, 8.8 us)
Async XLA Ops:
  0.6 33.2 %copy-start.2 = (bf16[512,1024]{1,0:T(8,128)(2,1)S(1)}, bf16[512,1024]{1,0:T(8,128)(2,1)}, u32[]{:S(2)}) copy-start(bf16[512,1024]{1,0:T(8,128)(2,1)} %wkv_ref.1) | copy-start | bytes 3145732
  0.6 33.2 %copy-start.4 = (bf16[512,512]{1,0:T(8,128)(2,1)S(1)}, bf16[512,512]{1,0:T(8,128)(2,1)}, u32[]{:S(2)}) copy-start(bf16[512,512]{1,0:T(8,128)(2,1)} %wq_ref.1) | copy-start | bytes 1572868
  0.7 33.2 %copy-start.7 = (f32[512]{0:T(512)S(1)}, f32[512]{0:T(512)}, u32[]{:S(2)}) copy-start(f32[512]{0:T(512)} %param.14) | copy-start | bytes 6148
  1.5 8.3 %collective-permute-start.4 = (bf16[32,512]{1,0:T(8,128)(2,1)S(1)}, bf16[32,512]{1,0:T(8,128)(2,1)S(1)}, u32[]{:S(2)}, u32[]{:S(2)}) collective-permute-start(bf16[32,512]{1,0:T(8,128)(2,1)S(1)} %reshape.20.tokens_ref), channel_id=1, source_target_pairs={{0,1},{1,0},{2,3},{3,2},{4,5},{5,4},{6,7},{7,6},{8,9},{9,8},{10,11... | collective-permute-start | bytes 98312 | tf_op jit(solution)/shard_map/ppermute | solution.py:292
  4.9 4.9 %collective-permute-start = (bf16[32,512]{1,0:T(8,128)(2,1)S(1)}, bf16[32,512]{1,0:T(8,128)(2,1)S(1)}, u32[]{:S(2)}, u32[]{:S(2)}) collective-permute-start(bf16[32,512]{1,0:T(8,128)(2,1)S(1)} %reshape.20.tokens_ref), channel_id=1, source_target_pairs={{0,16},{1,17},{2,18},{3,19},{4,20},{5,21},{6,22},{7,23},{8,24},{9,... | collective-permute-start | bytes 98312 | tf_op jit(solution)/shard_map/ppermute | solution.py:292
  5.7 23.0 %collective-permute-start.14 = (bf16[2,64,128]{2,1,0:T(8,128)(2,1)S(1)}, bf16[2,64,128]{2,1,0:T(8,128)(2,1)S(1)}, u32[]{:S(2)}, u32[]{:S(2)}) collective-permute-start(bf16[2,64,128]{2,1,0:T(8,128)(2,1)S(1)} %get-tuple-element.16), channel_id=1, source_target_pairs={{0,16},{16,0},{32,48},{48,32},{64,80},{80,64},{96,112},{112,96},{1... | collective-permute-start | bytes 98312 | tf_op jit(solution)/shard_map/ppermute | solution.py:316
  6.3 22.4 %collective-permute-start.13 = (bf16[2,64,128]{2,1,0:T(8,128)(2,1)S(1)}, bf16[2,64,128]{2,1,0:T(8,128)(2,1)S(1)}, u32[]{:S(2)}, u32[]{:S(2)}) collective-permute-start(bf16[2,64,128]{2,1,0:T(8,128)(2,1)S(1)} %get-tuple-element.17), channel_id=1, source_target_pairs={{0,240},{16,32},{32,16},{48,64},{64,48},{80,96},{96,80},{112,128},... | collective-permute-start | bytes 98312 | tf_op jit(solution)/shard_map/ppermute | solution.py:317
  9.8 6.9 %collective-permute-start.5 = (bf16[64,512]{1,0:T(8,128)(2,1)S(1)}, bf16[64,512]{1,0:T(8,128)(2,1)S(1)}, u32[]{:S(2)}, u32[]{:S(2)}) collective-permute-start(bf16[64,512]{1,0:T(8,128)(2,1)S(1)} %get-tuple-element.33), channel_id=1, source_target_pairs={{0,3},{1,2},{2,1},{3,0},{4,7},{5,6},{6,5},{7,4},{8,11},{9,10},{10,... | collective-permute-start | bytes 196616 | tf_op jit(solution)/shard_map/ppermute | solution.py:292
  13.5 5.0 %collective-permute-start.1 = (bf16[64,512]{1,0:T(8,128)(2,1)S(1)}, bf16[64,512]{1,0:T(8,128)(2,1)S(1)}, u32[]{:S(2)}, u32[]{:S(2)}) collective-permute-start(bf16[64,512]{1,0:T(8,128)(2,1)S(1)} %get-tuple-element.34), channel_id=1, source_target_pairs={{0,32},{1,33},{2,34},{3,35},{4,36},{5,37},{6,38},{7,39},{8,40},{9,... | collective-permute-start | bytes 196616 | tf_op jit(solution)/shard_map/ppermute | solution.py:292
  18.6 7.8 %collective-permute-start.6 = (bf16[128,512]{1,0:T(8,128)(2,1)S(1)}, bf16[128,512]{1,0:T(8,128)(2,1)S(1)}, u32[]{:S(2)}, u32[]{:S(2)}) collective-permute-start(bf16[128,512]{1,0:T(8,128)(2,1)S(1)} %get-tuple-element.31), channel_id=1, source_target_pairs={{0,4},{1,5},{2,6},{3,7},{4,0},{5,1},{6,2},{7,3},{8,12},{9,13},{10,... | collective-permute-start | bytes 393224 | tf_op jit(solution)/shard_map/ppermute | solution.py:292
  19.2 5.4 %collective-permute-start.2 = (bf16[128,512]{1,0:T(8,128)(2,1)S(1)}, bf16[128,512]{1,0:T(8,128)(2,1)S(1)}, u32[]{:S(2)}, u32[]{:S(2)}) collective-permute-start(bf16[128,512]{1,0:T(8,128)(2,1)S(1)} %get-tuple-element.32), channel_id=1, source_target_pairs={{0,64},{1,65},{2,66},{3,67},{4,68},{5,69},{6,70},{7,71},{8,72},{9,... | collective-permute-start | bytes 393224 | tf_op jit(solution)/shard_map/ppermute | solution.py:292
  24.6 7.3 %collective-permute-start.3 = (bf16[256,512]{1,0:T(8,128)(2,1)S(1)}, bf16[256,512]{1,0:T(8,128)(2,1)S(1)}, u32[]{:S(2)}, u32[]{:S(2)}) collective-permute-start(bf16[256,512]{1,0:T(8,128)(2,1)S(1)} %constant_dynamic-update-slice_fusion.q0_ref), channel_id=1, source_target_pairs={{0,192},{1,193},{2,194},{3,195},{4,196},{5,197},{6,198},{7,199},{8... | collective-permute-start | bytes 786440 | tf_op jit(solution)/shard_map/ppermute | solution.py:292
  26.4 7.4 %collective-permute-start.7 = (bf16[256,512]{1,0:T(8,128)(2,1)S(1)}, bf16[256,512]{1,0:T(8,128)(2,1)S(1)}, u32[]{:S(2)}, u32[]{:S(2)}) collective-permute-start(bf16[256,512]{1,0:T(8,128)(2,1)S(1)} %constant_dynamic-update-slice_fusion.4.k0_ref), channel_id=1, source_target_pairs={{0,12},{1,13},{2,14},{3,15},{4,8},{5,9},{6,10},{7,11},{8,4},{9,5},... | collective-permute-start | bytes 786440 | tf_op jit(solution)/shard_map/ppermute | solution.py:292
  33.9 24.2 %copy-start = (bf16[128,64,128]{2,1,0:T(8,128)(2,1)S(1)}, bf16[128,64,128]{2,1,0:T(8,128)(2,1)}, u32[]{:S(2)}) copy-start(bf16[128,64,128]{2,1,0:T(8,128)(2,1)} %fine_ref.5) | copy-start | bytes 6291460
  33.9 24.2 %copy-start.1 = (bf16[2,3,3,128,128]{4,3,2,1,0:T(8,128)(2,1)S(1)}, bf16[2,3,3,128,128]{4,3,2,1,0:T(8,128)(2,1)}, u32[]{:S(2)}) copy-start(bf16[2,3,3,128,128]{4,3,2,1,0:T(8,128)(2,1)} %refs_2_.3) | copy-start | bytes 1769476
  33.9 24.2 %copy-start.6 = (f32[2,128]{1,0:T(2,128)S(1)}, f32[2,128]{1,0:T(2,128)}, u32[]{:S(2)}) copy-start(f32[2,128]{1,0:T(2,128)} %gains_ref.5) | copy-start | bytes 3076
  37.4 6.3 %collective-permute-start.8 = (bf16[256,640]{1,0:T(8,128)(2,1)S(1)}, bf16[256,640]{1,0:T(8,128)(2,1)S(1)}, u32[]{:S(2)}, u32[]{:S(2)}) collective-permute-start(bf16[256,640]{1,0:T(8,128)(2,1)S(1)} %get-tuple-element.9), channel_id=1, source_target_pairs={{0,16},{1,17},{2,18},{3,19},{4,20},{5,21},{6,22},{7,23},{8,24},{9,... | collective-permute-start | bytes 983048 | tf_op jit(solution)/shard_map/ppermute | solution.py:292
  37.7 9.8 %collective-permute-start.15 = (bf16[132,2,128]{2,1,0:T(2,128)(2,1)S(1)}, bf16[132,2,128]{2,1,0:T(2,128)(2,1)S(1)}, u32[]{:S(2)}, u32[]{:S(2)}) collective-permute-start(bf16[132,2,128]{2,1,0:T(2,128)(2,1)S(1)} %get-tuple-element.20), channel_id=1, source_target_pairs={{0,1},{1,0},{2,3},{3,2},{4,5},{5,4},{6,7},{7,6},{8,9},{9,8},{10,11... | collective-permute-start | bytes 202760 | tf_op jit(solution)/shard_map/ppermute | solution.py:325
  38.4 10.4 %collective-permute-start.16 = (bf16[132,2,128]{2,1,0:T(2,128)(2,1)S(1)}, bf16[132,2,128]{2,1,0:T(2,128)(2,1)S(1)}, u32[]{:S(2)}, u32[]{:S(2)}) collective-permute-start(bf16[132,2,128]{2,1,0:T(2,128)(2,1)S(1)} %get-tuple-element.21), channel_id=1, source_target_pairs={{1,2},{2,1},{3,4},{4,3},{5,6},{6,5},{7,8},{8,7},{9,10},{10,9},{11,... | collective-permute-start | bytes 202760 | tf_op jit(solution)/shard_map/ppermute | solution.py:326
  43.8 8.9 %collective-permute-start.9 = (bf16[128,640]{1,0:T(8,128)(2,1)S(1)}, bf16[128,640]{1,0:T(8,128)(2,1)S(1)}, u32[]{:S(2)}, u32[]{:S(2)}) collective-permute-start(bf16[128,640]{1,0:T(8,128)(2,1)S(1)} %get-tuple-element.11), channel_id=1, source_target_pairs={{0,32},{1,33},{2,34},{3,35},{4,36},{5,37},{6,38},{7,39},{8,40},{9,... | collective-permute-start | bytes 491528 | tf_op jit(solution)/shard_map/ppermute | solution.py:292
  53.0 16.0 %collective-permute-start.12 = (bf16[32,640]{1,0:T(8,128)(2,1)S(1)}, bf16[32,640]{1,0:T(8,128)(2,1)S(1)}, u32[]{:S(2)}, u32[]{:S(2)}) collective-permute-start(bf16[32,640]{1,0:T(8,128)(2,1)S(1)} %get-tuple-element.22), channel_id=1, source_target_pairs={{0,128},{1,129},{2,130},{3,131},{4,132},{5,133},{6,134},{7,135},{8... | collective-permute-start | bytes 122888 | tf_op jit(solution)/shard_map/ppermute | solution.py:292
  54.3 14.7 %collective-permute-start.11 = (bf16[32,640]{1,0:T(8,128)(2,1)S(1)}, bf16[32,640]{1,0:T(8,128)(2,1)S(1)}, u32[]{:S(2)}, u32[]{:S(2)}) collective-permute-start(bf16[32,640]{1,0:T(8,128)(2,1)S(1)} %get-tuple-element.23), channel_id=1, source_target_pairs={{0,192},{1,193},{2,194},{3,195},{4,196},{5,197},{6,198},{7,199},{8... | collective-permute-start | bytes 122888 | tf_op jit(solution)/shard_map/ppermute | solution.py:292
  55.2 13.8 %collective-permute-start.10 = (bf16[32,640]{1,0:T(8,128)(2,1)S(1)}, bf16[32,640]{1,0:T(8,128)(2,1)S(1)}, u32[]{:S(2)}, u32[]{:S(2)}) collective-permute-start(bf16[32,640]{1,0:T(8,128)(2,1)S(1)} %get-tuple-element.24), channel_id=1, source_target_pairs={{0,64},{1,65},{2,66},{3,67},{4,68},{5,69},{6,70},{7,71},{8,72},{9,... | collective-permute-start | bytes 122888 | tf_op jit(solution)/shard_map/ppermute | solution.py:292
  66.9 2.1 %copy-start.3 = (bf16[512,512]{1,0:T(8,128)(2,1)S(1)}, bf16[512,512]{1,0:T(8,128)(2,1)}, u32[]{:S(2)}) copy-start(bf16[512,512]{1,0:T(8,128)(2,1)} %wo_ref.1) | copy-start | bytes 1572868
  (1 other events, 2.1 us)
